TPU v7x, 32 devices: a whole 2x2x4 slice. The times are simulated.
32 devices in a mesh: seq: 8 (over z, y), tp: 4 (over x, core).
Axes of the slice: x: 2, y: 2, z: 4, core: 2. Of those that a mesh axis runs over, the one named last changes fastest.
Arguments:
- inner_x: bfloat16 [2048, 8192], P('seq', 'tp'), may hold values from -6 to 6
- in_b: bfloat16 [2048, 1024], P('seq', 'tp'), may hold values from -6 to 6
- in_c: bfloat16 [2048, 1024], P('seq', 'tp'), may hold values from -6 to 6
- log_decay: float32 [128, 2048], P('tp', 'seq'), may hold values from -2 to 0
- doc_lengths: int32 [4], replicated, may hold values from 1 to 1024, 2048 in all
- out_grad: bfloat16 [2048, 8192], P('seq', 'tp'), may hold values from -0.0016937256 to 0.0016937256
- w_b: bfloat16 [8192, 1024], P(None, 'tp'), may hold values from -0.09375 to 0.09375
- w_c: bfloat16 [8192, 1024], P(None, 'tp'), may hold values from -0.0625 to 0.0625
Outputs:
- grad_x: bfloat16 [2048, 8192], P('seq', 'tp')
- grad_input: bfloat16 [2048, 8192], P('seq', 'tp')
Inputs may be any that keep to these rules, and one draw needn't show every extreme that they name: `doc_lengths`: the lengths sum to 2048; the longest is exactly half of 2048.
All inputs are finite; a program needn't handle non-finite values.
Results may differ from a plain program's by a relative error of at most 0.023.
Values may be sent and summed in bfloat16 or wider, within the bound.
A program may use at most 128 MiB of HBM per device.

v0:
```python
import functools

import jax
import jax.numpy as jnp
from jax import lax
from jax.experimental import pallas as pl
from jax.experimental.pallas import tpu as pltpu
from jax.sharding import PartitionSpec as P

HEAD_DIM = 64
STATE = 128
SPAN = 128
LAG = 5
WAIT = 6
F32 = jnp.float32
BF16 = jnp.bfloat16
MESH = pl.DeviceIdType.MESH
SMEM = pl.BlockSpec(memory_space=pltpu.SMEM)
ANY = pl.BlockSpec(memory_space=pl.ANY)


def dot(a, b, a_dim, b_dim):
    return lax.dot_general(a, b, (((a_dim,), (b_dim,)), ((), ())), preferred_element_type=F32)


def doc_of(lens_ref, position):
    end = 0
    doc = jnp.zeros_like(position)
    for k in range(lens_ref.shape[0] - 1):
        end = end + lens_ref[k]
        doc = doc + (position >= end).astype(jnp.int32)
    return doc


def span_decays(lens_ref, log_ref, number):
    heads, tokens = log_ref.shape
    first = lax.axis_index("seq") * tokens + number * SPAN
    cumulative = log_ref[:, number * SPAN : (number + 1) * SPAN]
    lane = lax.broadcasted_iota(jnp.int32, (heads, SPAN), 1)
    shift = 1
    while shift < SPAN:
        rolled = pltpu.roll(cumulative, shift, 1)
        cumulative = cumulative + jnp.where(lane >= shift, rolled, 0.0)
        shift *= 2
    doc_row = doc_of(lens_ref, first + lane)
    doc_last = doc_of(lens_ref, jnp.full((heads, SPAN), first + SPAN - 1, jnp.int32))
    before = jnp.full((heads, SPAN), first - 1, jnp.int32)
    doc_prior = jnp.where(before >= 0, doc_of(lens_ref, before), -1)
    last = jnp.broadcast_to(cumulative[:, SPAN - 1 :], (heads, SPAN))
    enter = jnp.where(doc_row == doc_prior, jnp.exp(cumulative), 0.0)
    leave = jnp.where(doc_row == doc_last, jnp.exp(last - cumulative), 0.0)
    total = jnp.where(doc_last == doc_prior, jnp.exp(last), 0.0)
    return cumulative, enter, leave, total


def fused_kernel(
    columns, chips, pieces, lens_ref, x_hbm, dy_hbm, b_hbm, c_hbm, log_hbm, wb_ref, wc_ref, gx_hbm, gi_hbm,
    x_ref, dy_ref, b_ref, c_ref, log_ref, turned, totals, d_ref, d_prev, d_next, bias, scores, mixed,
    xw_ref, dyw_ref, gx_local, gx_ref, gb_ref, gc_ref, gbc_ref, f0_ref, f_ref, g1_ref, g_ref,
    c_in, c_out, c_side, b_in, b_out, b_side,
    w_all, pair_out, pair_in, chip_out, chip_in, out_ref,
    load_sems, store_sems, d_sems, send_sems, recv_sems,
    w_sems, pair_send, pair_recv, chip_send, chip_recv,
):
    heads = log_ref.shape[0]
    groups = b_ref.shape[1] // STATE
    chunks = heads // 2
    pairs = chunks // groups
    width = 2 * HEAD_DIM
    k = lax.axis_index("seq")
    m = k // 2
    r = k - 2 * m
    devices = 2 * columns
    partner = k + 1 - 2 * r
    t = lax.axis_index("tp")
    chip = t // 2
    core = t - 2 * chip
    mate = t + 1 - 2 * core
    block = out_ref.shape[1]
    piece = block // pieces
    depth = wb_ref.shape[1]

    barrier = pltpu.get_barrier_semaphore()
    for offset in (-2, -1, 1, 2):
        @pl.when(jnp.logical_and(k + offset >= 0, k + offset < devices))
        def _():
            pl.semaphore_signal(
                barrier, inc=1, device_id={"seq": k + offset, "tp": t}, device_id_type=MESH
            )

    def owner_of(offset, same_core):
        at = lax.rem(chip + offset, chips)
        return 2 * at + (core if same_core else 1 - core)

    pl.semaphore_signal(barrier, inc=1, device_id={"seq": k, "tp": mate}, device_id_type=MESH)
    for offset in range(1, chips):
        pl.semaphore_signal(
            barrier, inc=1, device_id={"seq": k, "tp": owner_of(offset, True)}, device_id_type=MESH
        )

    quarter = x_ref.shape[1] // 4
    loads = [
        pltpu.make_async_copy(log_hbm, log_ref, load_sems.at[0]),
        pltpu.make_async_copy(b_hbm, b_ref, load_sems.at[1]),
        pltpu.make_async_copy(c_hbm, c_ref, load_sems.at[2]),
    ]
    for q in range(4):
        cols = pl.ds(q * quarter, quarter)
        loads.append(pltpu.make_async_copy(x_hbm.at[:, cols], x_ref.at[:, cols], load_sems.at[3 + 2 * q]))
        loads.append(pltpu.make_async_copy(dy_hbm.at[:, cols], dy_ref.at[:, cols], load_sems.at[4 + 2 * q]))
    for load in loads:
        load.start()

    def w_copy(offset, same_core, c, which):
        at = pl.multiple_of(owner_of(offset, same_core) * block + c * piece, piece)
        slot = (offset * 2 + (1 if same_core else 0)) * pieces + c
        return pltpu.make_async_copy(
            (wb_ref, wc_ref)[which].at[pl.ds(at, piece)],
            w_all.at[slot, :, pl.ds(which * depth, depth)],
            w_sems.at[slot, which],
        )

    for offset in range(chips):
        def fetch(c, carry):
            for same_core in (False, True):
                for which in (0, 1):
                    w_copy(offset, same_core, c, which).start()
            return carry

        lax.fori_loop(0, pieces, fetch, 0)

    loads[0].wait()
    low = lax.broadcasted_iota(jnp.int32, (SPAN, width), 1) < HEAD_DIM
    low_mask = low.astype(F32).astype(BF16)
    high_mask = (1.0 - low.astype(F32)).astype(BF16)
    row_id = lax.broadcasted_iota(jnp.int32, (SPAN, SPAN), 0)
    col_id = lax.broadcasted_iota(jnp.int32, (SPAN, SPAN), 1)
    for number in range(2):
        cumulative, enter, leave, total = span_decays(lens_ref, log_ref, number)
        log_ref[:, number * SPAN : (number + 1) * SPAN] = cumulative
        turned[3 * number] = jnp.transpose(cumulative)
        turned[3 * number + 1] = jnp.transpose(enter)
        turned[3 * number + 2] = jnp.transpose(leave)
        totals[number] = total
        first = k * log_ref.shape[1] + number * SPAN
        same = jnp.logical_and(
            doc_of(lens_ref, first + row_id) == doc_of(lens_ref, first + col_id), row_id >= col_id
        )
        bias[number] = jnp.where(same, 0.0, -1e30)
    both = totals[0] * totals[1]
    for h in range(heads):
        d_ref[h] = both[h : h + 1, :]

    count = jnp.minimum(k, 2) + jnp.minimum(devices - 1 - k, 2) + chips
    pl.semaphore_wait(barrier, count)

    def copy(stream, c, source, target, to):
        rows = pl.ds(pl.multiple_of(c * width, width), width)
        return pltpu.make_async_remote_copy(
            src_ref=source.at[rows], dst_ref=target.at[rows],
            send_sem=send_sems.at[stream, c], recv_sem=recv_sems.at[stream, c],
            device_id={"seq": to, "tp": t}, device_id_type=MESH,
        )

    def decay_copy(stream, target, to):
        return pltpu.make_async_remote_copy(
            src_ref=d_ref, dst_ref=target,
            send_sem=d_sems.at[0, stream], recv_sem=d_sems.at[1, stream],
            device_id={"seq": to, "tp": t}, device_id_type=MESH,
        )

    to_next = decay_copy(0, d_prev, k + 1)
    to_prev = decay_copy(1, d_next, k - 1)
    sends_next = jnp.logical_and(k + 1 >= 2, k + 1 < devices)
    sends_prev = jnp.logical_and(k >= 1, k - 1 <= devices - 3)

    @pl.when(sends_next)
    def _():
        to_next.start()

    @pl.when(sends_prev)
    def _():
        to_prev.start()

    loads[1].wait()
    loads[2].wait()

    def spans(number):
        return slice(number * SPAN, (number + 1) * SPAN)

    def spread(kind, number, pair):
        held = turned.at[3 * number + kind]
        one = jnp.broadcast_to(held[:, 2 * pair : 2 * pair + 1], (SPAN, width))
        two = jnp.broadcast_to(held[:, 2 * pair + 1 : 2 * pair + 2], (SPAN, width))
        return jnp.where(low, one, two)

    def by_head(number, pair):
        return jnp.concatenate(
            [
                jnp.broadcast_to(totals[number, h : h + 1, :], (HEAD_DIM, STATE))
                for h in (2 * pair, 2 * pair + 1)
            ],
            axis=0,
        )

    def summarize(pair):
        group = pair // pairs
        cols = slice(pair * width, (pair + 1) * width)
        cols_g = slice(group * STATE, (group + 1) * STATE)
        states, grads = [], []
        for number in (0, 1):
            tokens = spans(number)
            x_weighted = (x_ref[tokens, cols].astype(F32) * spread(2, number, pair)).astype(BF16)
            dy_weighted = (dy_ref[tokens, cols].astype(F32) * spread(1, number, pair)).astype(BF16)
            xw_ref[tokens, cols] = x_weighted
            dyw_ref[tokens, cols] = dy_weighted
            states.append(dot(x_weighted, b_ref[tokens, cols_g], 0, 0))
            grads.append(dot(dy_weighted, c_ref[tokens, cols_g], 0, 0))
        f0_ref[cols] = states[0]
        f_ref[cols] = states[1] + by_head(1, pair) * states[0]
        g1_ref[cols] = grads[1]
        g_ref[cols] = grads[0] + by_head(0, pair) * grads[1]

    def local(pair):
        group = pair // pairs
        cols = slice(pair * width, (pair + 1) * width)
        cols_g = slice(group * STATE, (group + 1) * STATE)
        for number in (0, 1):
            tokens = spans(number)
            slot = 2 * group + number
            if pair == group * pairs:
                scores[slot] = dot(c_ref[tokens, cols_g], b_ref[tokens, cols_g], 1, 1)
            x_part, dy_part = x_ref[tokens, cols], dy_ref[tokens, cols]
            x_blocks = jnp.concatenate([x_part * low_mask, x_part * high_mask], axis=0)
            dy_blocks = jnp.concatenate([dy_part * low_mask, dy_part * high_mask], axis=0)
            dots = dot(dy_part, x_blocks, 1, 1)
            score_low = []
            added = None
            for e in range(2):
                h = 2 * pair + e
                column = jnp.broadcast_to(turned[3 * number, :, h : h + 1], (SPAN, SPAN))
                gap = column - log_ref[h : h + 1, number * SPAN : (number + 1) * SPAN]
                within = jnp.exp(gap + bias[number])
                term = within * dots[:, e * SPAN : (e + 1) * SPAN]
                added = term if added is None else added + term
                score_low.append((within * scores[slot]).astype(BF16))
            mixed[slot] = added if pair == group * pairs else mixed[slot] + added
            gx_local[tokens, cols] = dot(jnp.concatenate(score_low, axis=0), dy_blocks, 0, 0)
            if pair == group * pairs + pairs - 1:
                mixed_low = mixed[slot].astype(BF16)
                gb_ref[tokens, cols_g] = dot(mixed_low, c_ref[tokens, cols_g], 0, 0)
                gc_ref[tokens, cols_g] = dot(mixed_low, b_ref[tokens, cols_g], 1, 0)

    def stream(base, has_in, has_next, ahead, source, buf_in, buf_out, buf_side, near, arrival, passes_own):
        chain = lambda c: copy(base, c, buf_out, buf_in, ahead)
        side_own = lambda c: copy(base + 1, c, buf_out, buf_side, partner)
        side_in = lambda c: copy(base + 1, c, buf_in, buf_side, partner)
        passes_in = jnp.logical_and(jnp.logical_not(passes_own), has_in)
        side_arrives = jnp.logical_or(jnp.logical_not(passes_own), has_in)

        def step(c):
            @pl.when(jnp.logical_and(has_in, c == 0))
            def _():
                arrival.wait_recv()

            @pl.when(has_in)
            def _():
                chain(c).wait_recv()

                @pl.when(jnp.logical_not(passes_own))
                def _():
                    side_in(c).start()

                for e in range(2):
                    h = 2 * c + e
                    rows = pl.ds(pl.multiple_of(h * HEAD_DIM, HEAD_DIM), HEAD_DIM)
                    product = d_ref[h] * near[h]
                    buf_out[rows, :] = (source[rows, :] + product * buf_in[rows, :].astype(F32)).astype(BF16)

            @pl.when(jnp.logical_not(has_in))
            def _():
                rows = pl.ds(pl.multiple_of(c * width, width), width)
                buf_out[rows, :] = source[rows, :].astype(BF16)

            @pl.when(passes_own)
            def _():
                side_own(c).start()

            @pl.when(has_next)
            def _():
                chain(c).start()

        def finish(c):
            @pl.when(side_arrives)
            def _():
                side_own(c).wait_recv()

            for e in range(2):
                h = 2 * c + e
                rows = slice(h * HEAD_DIM, (h + 1) * HEAD_DIM)

                @pl.when(has_in)
                def _():
                    source[rows, :] = (
                        buf_side[rows, :].astype(F32) + near[h] * buf_in[rows, :].astype(F32)
                    )

                @pl.when(jnp.logical_and(jnp.logical_not(has_in), side_arrives))
                def _():
                    source[rows, :] = buf_side[rows, :].astype(F32)

                @pl.when(jnp.logical_not(side_arrives))
                def _():
                    source[rows, :] = jnp.zeros((HEAD_DIM, STATE), F32)

        def drain(c):
            @pl.when(has_next)
            def _():
                chain(c).wait_send()

            @pl.when(jnp.logical_or(passes_own, passes_in))
            def _():
                side_own(c).wait_send()

        return step, finish, drain

    forward, forward_end, forward_drain = stream(
        0, m > 0, m < columns - 1, k + 2, f_ref, c_in, c_out, c_side, d_prev, to_next, r == 0
    )
    backward, backward_end, backward_drain = stream(
        2, m < columns - 1, m > 0, k - 2, g_ref, b_in, b_out, b_side, d_next, to_prev, r == 1
    )
    lead = LAG * (columns - 1 - 2 * m)
    forward_at = jnp.maximum(-lead, 0)
    backward_at = jnp.maximum(lead, 0)

    def carried(pair):
        group = pair // pairs
        cols = slice(pair * width, (pair + 1) * width)
        cols_g = slice(group * STATE, (group + 1) * STATE)
        forward_end(pair)
        backward_end(pair)
        arrived, ended = f_ref[cols], g_ref[cols]
        starts = [arrived.astype(BF16), (f0_ref[cols] + by_head(0, pair) * arrived).astype(BF16)]
        ends = [(g1_ref[cols] + by_head(1, pair) * ended).astype(BF16), ended.astype(BF16)]
        for number in (0, 1):
            tokens = spans(number)
            grad_x = gx_local[tokens, cols] + spread(2, number, pair) * dot(
                b_ref[tokens, cols_g], ends[number], 1, 1
            )
            gx_ref[tokens, cols] = grad_x.astype(BF16)
            gb_ref[tokens, cols_g] += dot(xw_ref[tokens, cols], ends[number], 1, 0)
            gc_ref[tokens, cols_g] += dot(dyw_ref[tokens, cols], starts[number], 1, 0)

    per_load = max(chunks // 4, 1)
    span_of_steps = LAG * (columns - 1)

    def exchange(s):
        f = s - forward_at
        b = s - backward_at

        @pl.when(jnp.logical_and(f >= 0, f < chunks))
        def _():
            forward(f)

        @pl.when(jnp.logical_and(b >= 0, b < chunks))
        def _():
            backward(b)

    for s in range(chunks + span_of_steps + WAIT):
        if s < chunks:
            if s % per_load == 0:
                loads[3 + 2 * (s // per_load)].wait()
                loads[4 + 2 * (s // per_load)].wait()
            summarize(s)
        if s < chunks + span_of_steps:
            exchange(s)
        if s < chunks:
            local(s)
        if s >= span_of_steps + WAIT:
            carried(s - span_of_steps - WAIT)
    gbc_ref[:, : groups * STATE] = gb_ref[...].astype(BF16)
    gbc_ref[:, groups * STATE :] = gc_ref[...].astype(BF16)
    store_x = pltpu.make_async_copy(gx_ref, gx_hbm, store_sems.at[0])
    store_x.start()

    def pair_copy(offset, c):
        slot = offset * pieces + c
        return pltpu.make_async_remote_copy(
            src_ref=pair_out.at[slot], dst_ref=pair_in.at[slot],
            send_sem=pair_send.at[slot], recv_sem=pair_recv.at[slot],
            device_id={"seq": k, "tp": mate}, device_id_type=MESH,
        )

    def chip_copy(offset, c):
        slot = (offset - 1) * pieces + c
        return pltpu.make_async_remote_copy(
            src_ref=chip_out.at[slot], dst_ref=chip_in.at[slot],
            send_sem=chip_send.at[slot], recv_sem=chip_recv.at[slot],
            device_id={"seq": k, "tp": owner_of(offset, True)}, device_id_type=MESH,
        )

    def partial(offset, same_core, c):
        for which in (0, 1):
            w_copy(offset, same_core, c, which).wait()
        slot = (offset * 2 + (1 if same_core else 0)) * pieces + c
        return dot(gbc_ref[...], w_all[slot], 1, 1)

    def give(offset, c):
        pair_out[offset * pieces + c] = partial(offset, False, c).astype(BF16)
        pair_copy(offset, c).start()

    def send_on(offset, c):
        own = partial(offset, True, c)
        pair_copy(offset, c).wait_recv()
        slot = offset * pieces + c
        chip_out[(offset - 1) * pieces + c] = (own + pair_in[slot].astype(F32)).astype(BF16)
        chip_copy(offset, c).start()

    for offset in range(1, chips):
        def body(s, carry):
            @pl.when(s < pieces)
            def _():
                give(offset, s)

            @pl.when(s >= 2)
            def _():
                send_on(offset, s - 2)

            return carry

        lax.fori_loop(0, pieces + 2, body, 0)

    def near_give(c, carry):
        give(0, c)
        return carry

    lax.fori_loop(0, pieces, near_give, 0)

    def final(c, carry):
        total = partial(0, True, c)
        pair_copy(0, c).wait_recv()
        total = total + pair_in[c].astype(F32)
        for offset in range(1, chips):
            chip_copy(offset, c).wait_recv()
            total = total + chip_in[(offset - 1) * pieces + c].astype(F32)
        cols = pl.ds(pl.multiple_of(c * piece, piece), piece)
        out_ref[:, cols] = total.astype(BF16)
        pltpu.make_async_copy(out_ref.at[:, cols], gi_hbm.at[:, cols], store_sems.at[1 + c]).start()
        return carry

    lax.fori_loop(0, pieces, final, 0)

    def drain(c, carry):
        for offset in range(chips):
            pair_copy(offset, c).wait_send()
        for offset in range(1, chips):
            chip_copy(offset, c).wait_send()
        cols = pl.ds(pl.multiple_of(c * piece, piece), piece)
        pltpu.make_async_copy(out_ref.at[:, cols], gi_hbm.at[:, cols], store_sems.at[1 + c]).wait()
        return carry

    lax.fori_loop(0, pieces, drain, 0)

    def drain_scan(c, carry):
        forward_drain(c)
        backward_drain(c)
        return carry

    lax.fori_loop(0, chunks, drain_scan, 0)

    @pl.when(sends_next)
    def _():
        to_next.wait_send()

    @pl.when(sends_prev)
    def _():
        to_prev.wait_send()

    store_x.wait()


def per_device(inner_x, in_b, in_c, log_decay, doc_lengths, out_grad, w_b, w_c):
    tokens, inner = inner_x.shape
    heads = log_decay.shape[0]
    seq_count, tp_count = lax.axis_size("seq"), lax.axis_size("tp")
    block = w_b.shape[0] // tp_count
    chips = tp_count // 2
    piece = 256
    pieces = block // piece
    chunks = heads // 2
    wide = in_b.shape[1]
    groups = wide // STATE
    vmem = pltpu.VMEM
    dma = pltpu.SemaphoreType.DMA
    row = vmem((heads, 1, STATE), F32)
    square = lambda n: vmem((n, SPAN, SPAN), F32)
    return tuple(pl.pallas_call(
        functools.partial(fused_kernel, seq_count // 2, chips, pieces),
        out_shape=[
            jax.ShapeDtypeStruct((tokens, inner), BF16),
            jax.ShapeDtypeStruct((tokens, block), BF16),
        ],
        in_specs=[SMEM] + [ANY] * 7,
        out_specs=[ANY] * 2,
        scratch_shapes=[
            vmem((tokens, inner), BF16), vmem((tokens, inner), BF16),
            vmem((tokens, wide), BF16), vmem((tokens, wide), BF16),
            vmem((heads, tokens), F32),
            vmem((6, SPAN, heads), F32), vmem((2, heads, SPAN), F32),
            row, row, row,
            square(2), square(2 * groups), square(2 * groups),
            vmem((tokens, inner), BF16), vmem((tokens, inner), BF16),
            vmem((tokens, inner), F32), vmem((tokens, inner), BF16),
            vmem((tokens, wide), F32), vmem((tokens, wide), F32), vmem((tokens, 2 * wide), BF16),
        ]
        + [vmem((inner, STATE), F32)] * 4
        + [vmem((inner, STATE), BF16)] * 6
        + [
            vmem((2 * chips * pieces, piece, 2 * wide), BF16),
            vmem((chips * pieces, tokens, piece), BF16),
            vmem((chips * pieces, tokens, piece), BF16),
            vmem(((chips - 1) * pieces, tokens, piece), BF16),
            vmem(((chips - 1) * pieces, tokens, piece), BF16),
            vmem((tokens, block), BF16),
            dma((11,)), dma((1 + pieces,)), dma((2, 2)), dma((4, chunks)), dma((4, chunks)),
            dma((2 * chips * pieces, 2)),
            dma((chips * pieces,)), dma((chips * pieces,)),
            dma(((chips - 1) * pieces,)), dma(((chips - 1) * pieces,)),
        ],
        compiler_params=pltpu.CompilerParams(
            collective_id=0, has_side_effects=True, vmem_limit_bytes=56 * 1024 * 1024
        ),
        name="fused",
    )(doc_lengths, inner_x, out_grad, in_b, in_c, log_decay, w_b, w_c))


def solution(mesh):
    placed = (
        P("seq", "tp"),
        P("seq", "tp"),
        P("seq", "tp"),
        P("tp", "seq"),
        P(),
        P("seq", "tp"),
        P(None, "tp"),
        P(None, "tp"),
    )
    return jax.shard_map(
        per_device,
        mesh=mesh,
        in_specs=placed,
        out_specs=(P("seq", "tp"), P("seq", "tp")),
        check_vma=False,
    )
```

profile of v0, /device:TPU:17, one launch (start us, length us, event | category | flops | bytes accessed | tf_op | source)
XLA Modules:
  0.0 66.7 jit_solution(14274514491363745148)
XLA Ops:
  0.6 61.5 %fused.1 = (bf16[256,2048]{1,0:T(8,128)(2,1)}, bf16[256,2048]{1,0:T(8,128)(2,1)}) custom-call(s32[4]{0:T(128)} %lens_ref.1, bf16[256,2048]{1,0:T(8,128)(2,1)} %x_hbm.1, bf16[256,2048]{1,0:T(8,128)(2,1)} %dy_hbm.1, bf16[256,256]{1,0:T(8,128)(2,1)} %b_hbm.1, bf16[256,256]{1,0:T(8,128)(2,1)} %c_hbm.1, f32[32,256]{1,0:T(8,128)} %log_hbm.1, ...), custom_call_target="tpu_custom_call" | custom-call | tf_op jit(solution)/shard_map/fused/pallas_call | solution.py:498
  62.1 2.3 %copy.12 = bf16[256,2048]{1,0:T(8,128)(2,1)} copy(bf16[256,2048]{1,0:T(8,128)(2,1)} %get-tuple-element.4) | data formatting | bytes 2097152
  64.4 2.3 %copy.13 = bf16[256,2048]{1,0:T(8,128)(2,1)} copy(bf16[256,2048]{1,0:T(8,128)(2,1)} %get-tuple-element.5) | data formatting | bytes 2097152
where the time goes:
time: 66.9 us; the launch traced here: 66.7 us
  Pallas kernels  61.5 us (92%)
  local copies, waits for them, and re-layouts  4.61 us (7%)
    pallas_call x1, Pallas kernels, per_device(): pl.pallas_call(functools.partial(fused_kernel, seq_count // 2, chips, pie...  61.5 us
    unnamed x2, local copies, waits for them, and re-layouts  4.61 us

commit v1 on v0

--- a/solution.py
+++ b/solution.py
@@ -54,12 +54,12 @@
 
 
 def fused_kernel(
-    columns, chips, pieces, lens_ref, x_hbm, dy_hbm, b_hbm, c_hbm, log_hbm, wb_ref, wc_ref, gx_hbm, gi_hbm,
+    columns, chips, pieces, lens_ref, x_hbm, dy_hbm, b_hbm, c_hbm, log_hbm, wb_ref, wc_ref, gx_ref, out_ref,
     x_ref, dy_ref, b_ref, c_ref, log_ref, turned, totals, d_ref, d_prev, d_next, bias, scores, mixed,
-    xw_ref, dyw_ref, gx_local, gx_ref, gb_ref, gc_ref, gbc_ref, f0_ref, f_ref, g1_ref, g_ref,
+    xw_ref, dyw_ref, gx_local, gb_ref, gc_ref, gbc_ref, f0_ref, f_ref, g1_ref, g_ref,
     c_in, c_out, c_side, b_in, b_out, b_side,
-    w_all, pair_out, pair_in, chip_out, chip_in, out_ref,
-    load_sems, store_sems, d_sems, send_sems, recv_sems,
+    w_all, pair_out, pair_in, chip_out, chip_in,
+    load_sems, d_sems, send_sems, recv_sems,
     w_sems, pair_send, pair_recv, chip_send, chip_recv,
 ):
     heads = log_ref.shape[0]
@@ -381,8 +381,6 @@
             carried(s - span_of_steps - WAIT)
     gbc_ref[:, : groups * STATE] = gb_ref[...].astype(BF16)
     gbc_ref[:, groups * STATE :] = gc_ref[...].astype(BF16)
-    store_x = pltpu.make_async_copy(gx_ref, gx_hbm, store_sems.at[0])
-    store_x.start()
 
     def pair_copy(offset, c):
         slot = offset * pieces + c
@@ -446,7 +444,6 @@
             total = total + chip_in[(offset - 1) * pieces + c].astype(F32)
         cols = pl.ds(pl.multiple_of(c * piece, piece), piece)
         out_ref[:, cols] = total.astype(BF16)
-        pltpu.make_async_copy(out_ref.at[:, cols], gi_hbm.at[:, cols], store_sems.at[1 + c]).start()
         return carry
 
     lax.fori_loop(0, pieces, final, 0)
@@ -456,8 +453,6 @@
             pair_copy(offset, c).wait_send()
         for offset in range(1, chips):
             chip_copy(offset, c).wait_send()
-        cols = pl.ds(pl.multiple_of(c * piece, piece), piece)
-        pltpu.make_async_copy(out_ref.at[:, cols], gi_hbm.at[:, cols], store_sems.at[1 + c]).wait()
         return carry
 
     lax.fori_loop(0, pieces, drain, 0)
@@ -476,8 +471,6 @@
     @pl.when(sends_prev)
     def _():
         to_prev.wait_send()
-
-    store_x.wait()
 
 
 def per_device(inner_x, in_b, in_c, log_decay, doc_lengths, out_grad, w_b, w_c):
@@ -498,11 +491,11 @@
     return tuple(pl.pallas_call(
         functools.partial(fused_kernel, seq_count // 2, chips, pieces),
         out_shape=[
-            jax.ShapeDtypeStruct((tokens, inner), BF16),
-            jax.ShapeDtypeStruct((tokens, block), BF16),
+            vmem((tokens, inner), BF16),
+            vmem((tokens, block), BF16),
         ],
         in_specs=[SMEM] + [ANY] * 7,
-        out_specs=[ANY] * 2,
+        out_specs=[pl.BlockSpec(memory_space=vmem)] * 2,
         scratch_shapes=[
             vmem((tokens, inner), BF16), vmem((tokens, inner), BF16),
             vmem((tokens, wide), BF16), vmem((tokens, wide), BF16),
@@ -511,7 +504,7 @@
             row, row, row,
             square(2), square(2 * groups), square(2 * groups),
             vmem((tokens, inner), BF16), vmem((tokens, inner), BF16),
-            vmem((tokens, inner), F32), vmem((tokens, inner), BF16),
+            vmem((tokens, inner), F32),
             vmem((tokens, wide), F32), vmem((tokens, wide), F32), vmem((tokens, 2 * wide), BF16),
         ]
         + [vmem((inner, STATE), F32)] * 4
@@ -522,8 +515,7 @@
             vmem((chips * pieces, tokens, piece), BF16),
             vmem(((chips - 1) * pieces, tokens, piece), BF16),
             vmem(((chips - 1) * pieces, tokens, piece), BF16),
-            vmem((tokens, block), BF16),
-            dma((11,)), dma((1 + pieces,)), dma((2, 2)), dma((4, chunks)), dma((4, chunks)),
+            dma((11,)), dma((2, 2)), dma((4, chunks)), dma((4, chunks)),
             dma((2 * chips * pieces, 2)),
             dma((chips * pieces,)), dma((chips * pieces,)),
             dma(((chips - 1) * pieces,)), dma(((chips - 1) * pieces,)),

time: 66.9 us -> 63.6 us (0.951)
  local copies, waits for them, and re-layouts: 4.61 us -> 1.94 us
  Pallas kernels: 61.5 us -> 60.8 us
    unnamed x2, local copies, waits for them, and re-layouts: 4.61 us -> 1.94 us
where the time goes in v1:
time: 63.6 us; the launch traced here: 63.4 us
  Pallas kernels  60.8 us (96%)
  local copies, waits for them, and re-layouts  1.94 us (3%)
  between operations  0.64 us (1%)
    pallas_call x1, Pallas kernels, per_device(): pl.pallas_call(functools.partial(fused_kernel, seq_count // 2, chips, pie...  60.8 us
    unnamed x2, local copies, waits for them, and re-layouts  1.94 us

profile of v1, /device:TPU:17, one launch (start us, length us, event | category | flops | bytes accessed | tf_op | source)
XLA Modules:
  0.0 63.4 jit_solution(17428756577441641944)
XLA Ops:
  0.6 60.8 %fused.1 = (bf16[256,2048]{1,0:T(8,128)(2,1)S(1)}, bf16[256,2048]{1,0:T(8,128)(2,1)S(1)}) custom-call(s32[4]{0:T(128)} %lens_ref.1, bf16[256,2048]{1,0:T(8,128)(2,1)} %x_hbm.1, bf16[256,2048]{1,0:T(8,128)(2,1)} %dy_hbm.1, bf16[256,256]{1,0:T(8,128)(2,1)} %b_hbm.1, bf16[256,256]{1,0:T(8,128)(2,1)} %c_hbm.1, f32[32,256]{1,0:T(8,128)} %log_hbm.1, ...), custom_call_target="tpu_custom_call" | custom-call | tf_op jit(solution)/shard_map/fused/pallas_call | solution.py:491
  61.5 1.0 %copy.12 = bf16[256,2048]{1,0:T(8,128)(2,1)} copy(bf16[256,2048]{1,0:T(8,128)(2,1)S(1)} %get-tuple-element.2) | data formatting | bytes 2097152
  62.5 1.0 %copy.13 = bf16[256,2048]{1,0:T(8,128)(2,1)} copy(bf16[256,2048]{1,0:T(8,128)(2,1)S(1)} %get-tuple-element.3) | data formatting | bytes 2097152

commit v2 on v1

--- a/solution.py
+++ b/solution.py
@@ -54,14 +54,18 @@
 
 
 def fused_kernel(
-    columns, chips, pieces, lens_ref, x_hbm, dy_hbm, b_hbm, c_hbm, log_hbm, wb_ref, wc_ref, gx_ref, out_ref,
+    columns, chips, pieces, whole, lens_ref, x_hbm, dy_hbm, b_hbm, c_hbm, log_hbm, wb_ref, wc_ref, gx_ref, out_ref,
     x_ref, dy_ref, b_ref, c_ref, log_ref, turned, totals, d_ref, d_prev, d_next, bias, scores, mixed,
     xw_ref, dyw_ref, gx_local, gb_ref, gc_ref, gbc_ref, f0_ref, f_ref, g1_ref, g_ref,
     c_in, c_out, c_side, b_in, b_out, b_side,
-    w_all, pair_out, pair_in, chip_out, chip_in,
+    w_own, w_far, pair_out, pair_in, chip_out, chip_in,
     load_sems, d_sems, send_sems, recv_sems,
-    w_sems, pair_send, pair_recv, chip_send, chip_recv,
+    w_sems, far_sems, pair_send, pair_recv, chip_send, chip_recv,
+    *shared,
 ):
+    summed = pieces - whole
+    if whole:
+        w_mate, w_cross, gbc_in, mate_sems, cross_sems, relay_sems, gbc_sems = shared
     heads = log_ref.shape[0]
     groups = b_ref.shape[1] // STATE
     chunks = heads // 2
@@ -79,6 +83,22 @@
     block = out_ref.shape[1]
     piece = block // pieces
     depth = wb_ref.shape[1]
+    z_at = m - 2 * (m // 2)
+    z_mate = k + 2 - 4 * z_at
+    here = 2 * z_at + r
+    over_y = 2 * z_at + 1 - r
+    over_z = 2 * (1 - z_at) + r
+    across = 2 * (1 - z_at) + 1 - r
+
+    def place(c):
+        if not whole:
+            return c
+        held = c // 4
+        pair_at = (c - 4 * held) // 2
+        odd = c - 2 * (c // 2)
+        added = (1 - pair_at) * (2 * across + odd) + pair_at * (2 * ((1 - odd) * over_y + odd * over_z) + 1)
+        gathered = (1 - pair_at) * (2 * here + odd) + pair_at * 2 * ((1 - odd) * over_y + odd * over_z)
+        return (1 - held) * added + held * gathered
 
     barrier = pltpu.get_barrier_semaphore()
     for offset in (-2, -1, 1, 2):
@@ -96,6 +116,10 @@
     for offset in range(1, chips):
         pl.semaphore_signal(
             barrier, inc=1, device_id={"seq": k, "tp": owner_of(offset, True)}, device_id_type=MESH
+        )
+    if whole:
+        pl.semaphore_signal(
+            barrier, inc=1, device_id={"seq": k, "tp": owner_of(1, False)}, device_id_type=MESH
         )
 
     quarter = x_ref.shape[1] // 4
@@ -111,23 +135,69 @@
     for load in loads:
         load.start()
 
+    def rows_of(offset, same_core, c):
+        at = owner_of(offset, same_core) * block + place(c) * piece
+        return pl.ds(pl.multiple_of(at, piece), piece)
+
+    def halves(which):
+        return pl.ds(which * depth, depth)
+
+    def far_slot(offset, same_core, c):
+        return (2 * offset - (1 if offset else 0) + (1 if same_core else 0)) * summed + c
+
     def w_copy(offset, same_core, c, which):
-        at = pl.multiple_of(owner_of(offset, same_core) * block + c * piece, piece)
-        slot = (offset * 2 + (1 if same_core else 0)) * pieces + c
+        own = offset == 0 and same_core
+        slot = c if own else far_slot(offset, same_core, c)
         return pltpu.make_async_copy(
-            (wb_ref, wc_ref)[which].at[pl.ds(at, piece)],
-            w_all.at[slot, :, pl.ds(which * depth, depth)],
-            w_sems.at[slot, which],
+            (wb_ref, wc_ref)[which].at[rows_of(offset, same_core, c)],
+            (w_own if own else w_far).at[slot, :, halves(which)],
+            (w_sems if own else far_sems).at[slot, which],
+        )
+
+    def mate_weights(g, which):
+        return pltpu.make_async_remote_copy(
+            src_ref=(wb_ref, wc_ref)[which].at[rows_of(0, False, summed + g)],
+            dst_ref=w_mate.at[g, :, halves(which)],
+            send_sem=mate_sems.at[0, g, which], recv_sem=mate_sems.at[1, g, which],
+            device_id={"seq": k, "tp": mate}, device_id_type=MESH,
+        )
+
+    def cross_weights(g, same_core, which):
+        source = 1 if same_core else 0
+        return pltpu.make_async_remote_copy(
+            src_ref=(wb_ref, wc_ref)[which].at[rows_of(1, same_core, summed + g)],
+            dst_ref=w_cross.at[source, g, :, halves(which)],
+            send_sem=cross_sems.at[0, source, g, which], recv_sem=cross_sems.at[1, source, g, which],
+            device_id={"seq": k, "tp": owner_of(1, same_core)}, device_id_type=MESH,
+        )
+
+    def relay_weights(axis, source):
+        return pltpu.make_async_remote_copy(
+            src_ref=w_cross.at[source, 0], dst_ref=w_cross.at[source, 2 + axis],
+            send_sem=relay_sems.at[0, axis, source], recv_sem=relay_sems.at[1, axis, source],
+            device_id={"seq": z_mate if axis else partner, "tp": t}, device_id_type=MESH,
+        )
+
+    def group_columns(group, half):
+        return pl.ds(half * groups * STATE + group * STATE, STATE)
+
+    def gbc_copy(kind, group, half):
+        cols = group_columns(group, half)
+        source = gbc_in.at[1] if kind == 2 else gbc_ref
+        return pltpu.make_async_remote_copy(
+            src_ref=source.at[:, cols], dst_ref=gbc_in.at[kind, :, cols],
+            send_sem=gbc_sems.at[0, kind, group, half], recv_sem=gbc_sems.at[1, kind, group, half],
+            device_id={"seq": k, "tp": owner_of(1, True) if kind == 1 else mate}, device_id_type=MESH,
         )
 
     for offset in range(chips):
-        def fetch(c, carry):
-            for same_core in (False, True):
+        for same_core in (False, True):
+            def fetch(c, carry):
                 for which in (0, 1):
                     w_copy(offset, same_core, c, which).start()
-            return carry
-
-        lax.fori_loop(0, pieces, fetch, 0)
+                return carry
+
+            lax.fori_loop(0, pieces if offset == 0 and same_core else summed, fetch, 0)
 
     loads[0].wait()
     low = lax.broadcasted_iota(jnp.int32, (SPAN, width), 1) < HEAD_DIM
@@ -151,7 +221,7 @@
     for h in range(heads):
         d_ref[h] = both[h : h + 1, :]
 
-    count = jnp.minimum(k, 2) + jnp.minimum(devices - 1 - k, 2) + chips
+    count = jnp.minimum(k, 2) + jnp.minimum(devices - 1 - k, 2) + chips + (1 if whole else 0)
     pl.semaphore_wait(barrier, count)
 
     def copy(stream, c, source, target, to):
@@ -181,6 +251,15 @@
     @pl.when(sends_prev)
     def _():
         to_prev.start()
+
+    if whole:
+        for g in range(2):
+            for which in (0, 1):
+                for same_core in (False, True):
+                    cross_weights(g, same_core, which).start()
+        for g in range(whole):
+            for which in (0, 1):
+                mate_weights(g, which).start()
 
     loads[1].wait()
     loads[2].wait()
@@ -351,6 +430,13 @@
             gx_ref[tokens, cols] = grad_x.astype(BF16)
             gb_ref[tokens, cols_g] += dot(xw_ref[tokens, cols], ends[number], 1, 0)
             gc_ref[tokens, cols_g] += dot(dyw_ref[tokens, cols], starts[number], 1, 0)
+        if pair == group * pairs + pairs - 1:
+            for half in (0, 1):
+                at = (half * groups + group) * STATE
+                gbc_ref[:, at : at + STATE] = (gc_ref if half else gb_ref)[:, cols_g].astype(BF16)
+                if whole:
+                    gbc_copy(1, group, half).start()
+                    gbc_copy(0, group, half).start()
 
     per_load = max(chunks // 4, 1)
     span_of_steps = LAG * (columns - 1)
@@ -379,11 +465,23 @@
             local(s)
         if s >= span_of_steps + WAIT:
             carried(s - span_of_steps - WAIT)
-    gbc_ref[:, : groups * STATE] = gb_ref[...].astype(BF16)
-    gbc_ref[:, groups * STATE :] = gc_ref[...].astype(BF16)
+
+    def relay_group(group):
+        for half in (0, 1):
+            gbc_copy(1, group, half).wait_recv()
+            gbc_copy(2, group, half).start()
+
+    if whole:
+        for source in (0, 1):
+            for which in (0, 1):
+                cross_weights(0, source == 1, which).wait_recv()
+            for axis in (0, 1):
+                relay_weights(axis, source).start()
+        for group in range(groups - 1):
+            relay_group(group)
 
     def pair_copy(offset, c):
-        slot = offset * pieces + c
+        slot = offset * summed + c
         return pltpu.make_async_remote_copy(
             src_ref=pair_out.at[slot], dst_ref=pair_in.at[slot],
             send_sem=pair_send.at[slot], recv_sem=pair_recv.at[slot],
@@ -391,7 +489,7 @@
         )
 
     def chip_copy(offset, c):
-        slot = (offset - 1) * pieces + c
+        slot = (offset - 1) * summed + c
         return pltpu.make_async_remote_copy(
             src_ref=chip_out.at[slot], dst_ref=chip_in.at[slot],
             send_sem=chip_send.at[slot], recv_sem=chip_recv.at[slot],
@@ -401,23 +499,23 @@
     def partial(offset, same_core, c):
         for which in (0, 1):
             w_copy(offset, same_core, c, which).wait()
-        slot = (offset * 2 + (1 if same_core else 0)) * pieces + c
-        return dot(gbc_ref[...], w_all[slot], 1, 1)
+        weights = w_own[c] if offset == 0 and same_core else w_far[far_slot(offset, same_core, c)]
+        return dot(gbc_ref[...], weights, 1, 1)
 
     def give(offset, c):
-        pair_out[offset * pieces + c] = partial(offset, False, c).astype(BF16)
+        pair_out[offset * summed + c] = partial(offset, False, c).astype(BF16)
         pair_copy(offset, c).start()
 
     def send_on(offset, c):
         own = partial(offset, True, c)
         pair_copy(offset, c).wait_recv()
-        slot = offset * pieces + c
-        chip_out[(offset - 1) * pieces + c] = (own + pair_in[slot].astype(F32)).astype(BF16)
+        slot = offset * summed + c
+        chip_out[(offset - 1) * summed + c] = (own + pair_in[slot].astype(F32)).astype(BF16)
         chip_copy(offset, c).start()
 
     for offset in range(1, chips):
         def body(s, carry):
-            @pl.when(s < pieces)
+            @pl.when(s < summed)
             def _():
                 give(offset, s)
 
@@ -427,13 +525,34 @@
 
             return carry
 
-        lax.fori_loop(0, pieces + 2, body, 0)
+        lax.fori_loop(0, summed + 2, body, 0)
 
     def near_give(c, carry):
         give(0, c)
         return carry
 
-    lax.fori_loop(0, pieces, near_give, 0)
+    lax.fori_loop(0, summed, near_give, 0)
+
+    def gather(g, carry):
+        for which in (0, 1):
+            w_copy(0, True, summed + g, which).wait()
+            mate_weights(g, which).wait_recv()
+        total = dot(gbc_ref[...], w_own[summed + g], 1, 1) + dot(gbc_in[0], w_mate[g], 1, 1)
+        total = total + dot(gbc_in[1], w_cross[1, g], 1, 1) + dot(gbc_in[2], w_cross[0, g], 1, 1)
+        cols = pl.ds(pl.multiple_of(place(summed + g) * piece, piece), piece)
+        out_ref[:, cols] = total.astype(BF16)
+        return carry
+
+    if whole:
+        relay_group(groups - 1)
+        for which in (0, 1):
+            for source in (0, 1):
+                cross_weights(1, source == 1, which).wait_recv()
+        for group in range(groups):
+            for half in (0, 1):
+                gbc_copy(0, group, half).wait_recv()
+                gbc_copy(2, group, half).wait_recv()
+        lax.fori_loop(0, 2, gather, 0)
 
     def final(c, carry):
         total = partial(0, True, c)
@@ -441,12 +560,19 @@
         total = total + pair_in[c].astype(F32)
         for offset in range(1, chips):
             chip_copy(offset, c).wait_recv()
-            total = total + chip_in[(offset - 1) * pieces + c].astype(F32)
-        cols = pl.ds(pl.multiple_of(c * piece, piece), piece)
+            total = total + chip_in[(offset - 1) * summed + c].astype(F32)
+        cols = pl.ds(pl.multiple_of(place(c) * piece, piece), piece)
         out_ref[:, cols] = total.astype(BF16)
         return carry
 
-    lax.fori_loop(0, pieces, final, 0)
+    early = summed - 1 if whole else summed
+    lax.fori_loop(0, early, final, 0)
+    if whole:
+        for axis in (0, 1):
+            for source in (0, 1):
+                relay_weights(axis, source).wait_recv()
+        lax.fori_loop(2, whole, gather, 0)
+        final(early, 0)
 
     def drain(c, carry):
         for offset in range(chips):
@@ -455,7 +581,22 @@
             chip_copy(offset, c).wait_send()
         return carry
 
-    lax.fori_loop(0, pieces, drain, 0)
+    lax.fori_loop(0, summed, drain, 0)
+
+    if whole:
+        for which in (0, 1):
+            for g in range(2):
+                for same_core in (False, True):
+                    cross_weights(g, same_core, which).wait_send()
+            for g in range(whole):
+                mate_weights(g, which).wait_send()
+        for axis in (0, 1):
+            for source in (0, 1):
+                relay_weights(axis, source).wait_send()
+        for kind in range(3):
+            for group in range(groups):
+                for half in (0, 1):
+                    gbc_copy(kind, group, half).wait_send()
 
     def drain_scan(c, carry):
         forward_drain(c)
@@ -483,13 +624,15 @@
     pieces = block // piece
     chunks = heads // 2
     wide = in_b.shape[1]
+    whole = 4 if chips == 2 and pieces == 8 and seq_count % 4 == 0 else 0
+    summed = pieces - whole
     groups = wide // STATE
     vmem = pltpu.VMEM
     dma = pltpu.SemaphoreType.DMA
     row = vmem((heads, 1, STATE), F32)
     square = lambda n: vmem((n, SPAN, SPAN), F32)
     return tuple(pl.pallas_call(
-        functools.partial(fused_kernel, seq_count // 2, chips, pieces),
+        functools.partial(fused_kernel, seq_count // 2, chips, pieces, whole),
         out_shape=[
             vmem((tokens, inner), BF16),
             vmem((tokens, block), BF16),
@@ -510,16 +653,23 @@
         + [vmem((inner, STATE), F32)] * 4
         + [vmem((inner, STATE), BF16)] * 6
         + [
-            vmem((2 * chips * pieces, piece, 2 * wide), BF16),
-            vmem((chips * pieces, tokens, piece), BF16),
-            vmem((chips * pieces, tokens, piece), BF16),
-            vmem(((chips - 1) * pieces, tokens, piece), BF16),
-            vmem(((chips - 1) * pieces, tokens, piece), BF16),
+            vmem((pieces, piece, 2 * wide), BF16),
+            vmem(((2 * chips - 1) * summed, piece, 2 * wide), BF16),
+            vmem((chips * summed, tokens, piece), BF16),
+            vmem((chips * summed, tokens, piece), BF16),
+            vmem(((chips - 1) * summed, tokens, piece), BF16),
+            vmem(((chips - 1) * summed, tokens, piece), BF16),
             dma((11,)), dma((2, 2)), dma((4, chunks)), dma((4, chunks)),
-            dma((2 * chips * pieces, 2)),
-            dma((chips * pieces,)), dma((chips * pieces,)),
-            dma(((chips - 1) * pieces,)), dma(((chips - 1) * pieces,)),
-        ],
+            dma((pieces, 2)), dma(((2 * chips - 1) * summed, 2)),
+            dma((chips * summed,)), dma((chips * summed,)),
+            dma(((chips - 1) * summed,)), dma(((chips - 1) * summed,)),
+        ]
+        + ([
+            vmem((whole, piece, 2 * wide), BF16),
+            vmem((2, whole, piece, 2 * wide), BF16),
+            vmem((3, tokens, 2 * wide), BF16),
+            dma((2, whole, 2)), dma((2, 2, 2, 2)), dma((2, 2, 2)), dma((2, 3, groups, 2)),
+        ] if whole else []),
         compiler_params=pltpu.CompilerParams(
             collective_id=0, has_side_effects=True, vmem_limit_bytes=56 * 1024 * 1024
         ),

time: 63.6 us -> 52.8 us (0.83)
  the two profiles are of different devices: /device:TPU:17 before, /device:TPU:0 now
where the time goes in v2:
time: 52.8 us; the launch traced here: 51.9 us
  Pallas kernels  49.3 us (93%)
  local copies, waits for them, and re-layouts  1.94 us (4%)
  between operations  0.64 us (1%)
    pallas_call x1, Pallas kernels, per_device(): pl.pallas_call(functools.partial(fused_kernel, seq_count // 2, chips, pie...  49.3 us
    unnamed x2, local copies, waits for them, and re-layouts  1.94 us

profile of v2, /device:TPU:0, one launch (start us, length us, event | category | flops | bytes accessed | tf_op | source)
XLA Modules:
  0.0 51.9 jit_solution(14383464608317085148)
XLA Ops:
  0.6 49.3 %fused.1 = (bf16[256,2048]{1,0:T(8,128)(2,1)S(1)}, bf16[256,2048]{1,0:T(8,128)(2,1)S(1)}) custom-call(s32[4]{0:T(128)} %lens_ref.1, bf16[256,2048]{1,0:T(8,128)(2,1)} %x_hbm.1, bf16[256,2048]{1,0:T(8,128)(2,1)} %dy_hbm.1, bf16[256,256]{1,0:T(8,128)(2,1)} %b_hbm.1, bf16[256,256]{1,0:T(8,128)(2,1)} %c_hbm.1, f32[32,256]{1,0:T(8,128)} %log_hbm.1, ...), custom_call_target="tpu_custom_call" | custom-call | tf_op jit(solution)/shard_map/fused/pallas_call | solution.py:634
  50.0 1.0 %copy.12 = bf16[256,2048]{1,0:T(8,128)(2,1)} copy(bf16[256,2048]{1,0:T(8,128)(2,1)S(1)} %get-tuple-element.2) | data formatting | bytes 2097152
  51.0 1.0 %copy.13 = bf16[256,2048]{1,0:T(8,128)(2,1)} copy(bf16[256,2048]{1,0:T(8,128)(2,1)S(1)} %get-tuple-element.3) | data formatting | bytes 2097152

commit v3 on v2

--- a/solution.py
+++ b/solution.py
@@ -60,7 +60,7 @@
     c_in, c_out, c_side, b_in, b_out, b_side,
     w_own, w_far, pair_out, pair_in, chip_out, chip_in,
     load_sems, d_sems, send_sems, recv_sems,
-    w_sems, far_sems, pair_send, pair_recv, chip_send, chip_recv,
+    w_sems, pair_send, pair_recv, chip_send, chip_recv,
     *shared,
 ):
     summed = pieces - whole
@@ -151,14 +151,14 @@
         return pltpu.make_async_copy(
             (wb_ref, wc_ref)[which].at[rows_of(offset, same_core, c)],
             (w_own if own else w_far).at[slot, :, halves(which)],
-            (w_sems if own else far_sems).at[slot, which],
+            w_sems.at[0 if own else 1],
         )
 
     def mate_weights(g, which):
         return pltpu.make_async_remote_copy(
             src_ref=(wb_ref, wc_ref)[which].at[rows_of(0, False, summed + g)],
             dst_ref=w_mate.at[g, :, halves(which)],
-            send_sem=mate_sems.at[0, g, which], recv_sem=mate_sems.at[1, g, which],
+            send_sem=mate_sems.at[0], recv_sem=mate_sems.at[1],
             device_id={"seq": k, "tp": mate}, device_id_type=MESH,
         )
 
@@ -167,14 +167,14 @@
         return pltpu.make_async_remote_copy(
             src_ref=(wb_ref, wc_ref)[which].at[rows_of(1, same_core, summed + g)],
             dst_ref=w_cross.at[source, g, :, halves(which)],
-            send_sem=cross_sems.at[0, source, g, which], recv_sem=cross_sems.at[1, source, g, which],
+            send_sem=cross_sems.at[0], recv_sem=cross_sems.at[1 + g],
             device_id={"seq": k, "tp": owner_of(1, same_core)}, device_id_type=MESH,
         )
 
     def relay_weights(axis, source):
         return pltpu.make_async_remote_copy(
             src_ref=w_cross.at[source, 0], dst_ref=w_cross.at[source, 2 + axis],
-            send_sem=relay_sems.at[0, axis, source], recv_sem=relay_sems.at[1, axis, source],
+            send_sem=relay_sems.at[0], recv_sem=relay_sems.at[1 + axis],
             device_id={"seq": z_mate if axis else partner, "tp": t}, device_id_type=MESH,
         )
 
@@ -186,7 +186,7 @@
         source = gbc_in.at[1] if kind == 2 else gbc_ref
         return pltpu.make_async_remote_copy(
             src_ref=source.at[:, cols], dst_ref=gbc_in.at[kind, :, cols],
-            send_sem=gbc_sems.at[0, kind, group, half], recv_sem=gbc_sems.at[1, kind, group, half],
+            send_sem=gbc_sems.at[0], recv_sem=gbc_sems.at[3 + group if kind == 1 else 1 + kind // 2],
             device_id={"seq": k, "tp": owner_of(1, True) if kind == 1 else mate}, device_id_type=MESH,
         )
 
@@ -228,9 +228,12 @@
         rows = pl.ds(pl.multiple_of(c * width, width), width)
         return pltpu.make_async_remote_copy(
             src_ref=source.at[rows], dst_ref=target.at[rows],
-            send_sem=send_sems.at[stream, c], recv_sem=recv_sems.at[stream, c],
+            send_sem=send_sems.at[stream], recv_sem=recv_sems.at[stream, c],
             device_id={"seq": to, "tp": t}, device_id_type=MESH,
         )
+
+    def settle(held, sem):
+        pltpu.make_async_copy(held, held, sem).wait()
 
     def decay_copy(stream, target, to):
         return pltpu.make_async_remote_copy(
@@ -392,14 +395,14 @@
                 def _():
                     source[rows, :] = jnp.zeros((HEAD_DIM, STATE), F32)
 
-        def drain(c):
+        def drain():
             @pl.when(has_next)
             def _():
-                chain(c).wait_send()
+                settle(buf_out, send_sems.at[base])
 
             @pl.when(jnp.logical_or(passes_own, passes_in))
             def _():
-                side_own(c).wait_send()
+                settle(buf_out, send_sems.at[base + 1])
 
         return step, finish, drain
 
@@ -467,14 +470,16 @@
             carried(s - span_of_steps - WAIT)
 
     def relay_group(group):
+        settle(gbc_in.at[1, :, pl.ds(0, 2 * STATE)], gbc_sems.at[3 + group])
         for half in (0, 1):
-            gbc_copy(1, group, half).wait_recv()
             gbc_copy(2, group, half).start()
 
+    settle(w_own, w_sems.at[0])
+    settle(w_far, w_sems.at[1])
+
     if whole:
+        settle(w_cross.at[:, 0], cross_sems.at[1])
         for source in (0, 1):
-            for which in (0, 1):
-                cross_weights(0, source == 1, which).wait_recv()
             for axis in (0, 1):
                 relay_weights(axis, source).start()
         for group in range(groups - 1):
@@ -484,7 +489,7 @@
         slot = offset * summed + c
         return pltpu.make_async_remote_copy(
             src_ref=pair_out.at[slot], dst_ref=pair_in.at[slot],
-            send_sem=pair_send.at[slot], recv_sem=pair_recv.at[slot],
+            send_sem=pair_send.at[0], recv_sem=pair_recv.at[slot],
             device_id={"seq": k, "tp": mate}, device_id_type=MESH,
         )
 
@@ -492,13 +497,11 @@
         slot = (offset - 1) * summed + c
         return pltpu.make_async_remote_copy(
             src_ref=chip_out.at[slot], dst_ref=chip_in.at[slot],
-            send_sem=chip_send.at[slot], recv_sem=chip_recv.at[slot],
+            send_sem=chip_send.at[0], recv_sem=chip_recv.at[slot],
             device_id={"seq": k, "tp": owner_of(offset, True)}, device_id_type=MESH,
         )
 
     def partial(offset, same_core, c):
-        for which in (0, 1):
-            w_copy(offset, same_core, c, which).wait()
         weights = w_own[c] if offset == 0 and same_core else w_far[far_slot(offset, same_core, c)]
         return dot(gbc_ref[...], weights, 1, 1)
 
@@ -534,9 +537,6 @@
     lax.fori_loop(0, summed, near_give, 0)
 
     def gather(g, carry):
-        for which in (0, 1):
-            w_copy(0, True, summed + g, which).wait()
-            mate_weights(g, which).wait_recv()
         total = dot(gbc_ref[...], w_own[summed + g], 1, 1) + dot(gbc_in[0], w_mate[g], 1, 1)
         total = total + dot(gbc_in[1], w_cross[1, g], 1, 1) + dot(gbc_in[2], w_cross[0, g], 1, 1)
         cols = pl.ds(pl.multiple_of(place(summed + g) * piece, piece), piece)
@@ -545,13 +545,10 @@
 
     if whole:
         relay_group(groups - 1)
-        for which in (0, 1):
-            for source in (0, 1):
-                cross_weights(1, source == 1, which).wait_recv()
-        for group in range(groups):
-            for half in (0, 1):
-                gbc_copy(0, group, half).wait_recv()
-                gbc_copy(2, group, half).wait_recv()
+        settle(w_mate, mate_sems.at[1])
+        settle(w_cross.at[:, 1], cross_sems.at[2])
+        settle(gbc_in.at[0], gbc_sems.at[1])
+        settle(gbc_in.at[2], gbc_sems.at[2])
         lax.fori_loop(0, 2, gather, 0)
 
     def final(c, carry):
@@ -569,41 +566,19 @@
     lax.fori_loop(0, early, final, 0)
     if whole:
         for axis in (0, 1):
-            for source in (0, 1):
-                relay_weights(axis, source).wait_recv()
+            settle(w_cross.at[:, 2 + axis], relay_sems.at[1 + axis])
         lax.fori_loop(2, whole, gather, 0)
         final(early, 0)
 
-    def drain(c, carry):
-        for offset in range(chips):
-            pair_copy(offset, c).wait_send()
-        for offset in range(1, chips):
-            chip_copy(offset, c).wait_send()
-        return carry
-
-    lax.fori_loop(0, summed, drain, 0)
-
+    settle(pair_out, pair_send.at[0])
+    settle(chip_out, chip_send.at[0])
     if whole:
-        for which in (0, 1):
-            for g in range(2):
-                for same_core in (False, True):
-                    cross_weights(g, same_core, which).wait_send()
-            for g in range(whole):
-                mate_weights(g, which).wait_send()
-        for axis in (0, 1):
-            for source in (0, 1):
-                relay_weights(axis, source).wait_send()
-        for kind in range(3):
-            for group in range(groups):
-                for half in (0, 1):
-                    gbc_copy(kind, group, half).wait_send()
-
-    def drain_scan(c, carry):
-        forward_drain(c)
-        backward_drain(c)
-        return carry
-
-    lax.fori_loop(0, chunks, drain_scan, 0)
+        settle(w_cross.at[:, pl.ds(0, 2)], cross_sems.at[0])
+        settle(w_mate, mate_sems.at[0])
+        settle(w_cross.at[:, pl.ds(0, 2)], relay_sems.at[0])
+        settle(gbc_in, gbc_sems.at[0])
+    forward_drain()
+    backward_drain()
 
     @pl.when(sends_next)
     def _():
@@ -612,6 +587,19 @@
     @pl.when(sends_prev)
     def _():
         to_prev.wait_send()
+
+
+def store_kernel(x_ref, input_ref, x_hbm, input_hbm, sems):
+    copies = []
+    for i, (held, target) in enumerate(((x_ref, x_hbm), (input_ref, input_hbm))):
+        part = held.shape[0] // 4
+        for n in range(4):
+            rows = pl.ds(n * part, part)
+            copies.append(pltpu.make_async_copy(held.at[rows], target.at[rows], sems.at[i, n]))
+    for copy in copies:
+        copy.start()
+    for copy in copies:
+        copy.wait()
 
 
 def per_device(inner_x, in_b, in_c, log_decay, doc_lengths, out_grad, w_b, w_c):
@@ -631,7 +619,7 @@
     dma = pltpu.SemaphoreType.DMA
     row = vmem((heads, 1, STATE), F32)
     square = lambda n: vmem((n, SPAN, SPAN), F32)
-    return tuple(pl.pallas_call(
+    held_x, held_input = pl.pallas_call(
         functools.partial(fused_kernel, seq_count // 2, chips, pieces, whole),
         out_shape=[
             vmem((tokens, inner), BF16),
@@ -659,22 +647,31 @@
             vmem((chips * summed, tokens, piece), BF16),
             vmem(((chips - 1) * summed, tokens, piece), BF16),
             vmem(((chips - 1) * summed, tokens, piece), BF16),
-            dma((11,)), dma((2, 2)), dma((4, chunks)), dma((4, chunks)),
-            dma((pieces, 2)), dma(((2 * chips - 1) * summed, 2)),
-            dma((chips * summed,)), dma((chips * summed,)),
-            dma(((chips - 1) * summed,)), dma(((chips - 1) * summed,)),
+            dma((11,)), dma((2, 2)), dma((4,)), dma((4, chunks)),
+            dma((2,)), dma((1,)), dma((chips * summed,)), dma((1,)), dma(((chips - 1) * summed,)),
         ]
         + ([
             vmem((whole, piece, 2 * wide), BF16),
             vmem((2, whole, piece, 2 * wide), BF16),
             vmem((3, tokens, 2 * wide), BF16),
-            dma((2, whole, 2)), dma((2, 2, 2, 2)), dma((2, 2, 2)), dma((2, 3, groups, 2)),
+            dma((2,)), dma((3,)), dma((3,)), dma((3 + groups,)),
         ] if whole else []),
         compiler_params=pltpu.CompilerParams(
             collective_id=0, has_side_effects=True, vmem_limit_bytes=56 * 1024 * 1024
         ),
         name="fused",
-    )(doc_lengths, inner_x, out_grad, in_b, in_c, log_decay, w_b, w_c))
+    )(doc_lengths, inner_x, out_grad, in_b, in_c, log_decay, w_b, w_c)
+    return tuple(pl.pallas_call(
+        store_kernel,
+        out_shape=[
+            jax.ShapeDtypeStruct((tokens, inner), BF16),
+            jax.ShapeDtypeStruct((tokens, block), BF16),
+        ],
+        in_specs=[pl.BlockSpec(memory_space=vmem)] * 2,
+        out_specs=[ANY] * 2,
+        scratch_shapes=[dma((2, 4))],
+        name="store",
+    )(pltpu.with_memory_space_constraint(held_x, pltpu.VMEM), pltpu.with_memory_space_constraint(held_input, pltpu.VMEM)))
 
 
 def solution(mesh):

time: 52.8 us -> 50.7 us (0.960)
  local copies, waits for them, and re-layouts: 1.94 us -> 0 us
    unnamed x2 -> x0, local copies, waits for them, and re-layouts: 1.94 us -> none
    pallas_call x1, Pallas kernels: 49.3 us -> 47.6 us  [per_device(): pl.pallas_call(functools.partial(fused_kernel, seq_count // 2, chips, pie...]
    pallas_call x0 -> x1, Pallas kernels: none -> 1.38 us  [per_device(): pl.pallas_call(store_kernel, out_shape=[jax.ShapeDtypeStruct((tokens, inn...]
where the time goes in v3:
time: 50.7 us; the launch traced here: 49.8 us
  Pallas kernels  49 us (97%)
  between operations  0.8 us (2%)
    pallas_call x1, Pallas kernels, per_device(): pl.pallas_call(functools.partial(fused_kernel, seq_count // 2, chips, pie...  47.6 us
    pallas_call x1, Pallas kernels, per_device(): pl.pallas_call(store_kernel, out_shape=[jax.ShapeDtypeStruct((tokens, inn...  1.38 us

profile of v3, /device:TPU:0, one launch (start us, length us, event | category | flops | bytes accessed | tf_op | source)
XLA Modules:
  0.0 49.8 jit_solution(16725696827606919608)
XLA Ops:
  0.6 47.6 %fused.1 = (bf16[256,2048]{1,0:T(8,128)(2,1)S(1)}, bf16[256,2048]{1,0:T(8,128)(2,1)S(1)}) custom-call(s32[4]{0:T(128)} %lens_ref.1, bf16[256,2048]{1,0:T(8,128)(2,1)} %x_hbm.1, bf16[256,2048]{1,0:T(8,128)(2,1)} %dy_hbm.1, bf16[256,256]{1,0:T(8,128)(2,1)} %b_hbm.1, bf16[256,256]{1,0:T(8,128)(2,1)} %c_hbm.1, f32[32,256]{1,0:T(8,128)} %log_hbm.1, ...), custom_call_target="tpu_custom_call" | custom-call | tf_op jit(solution)/shard_map/fused/pallas_call | solution.py:622
  48.3 1.4 %store.1 = (bf16[256,2048]{1,0:T(8,128)(2,1)}, bf16[256,2048]{1,0:T(8,128)(2,1)}) custom-call(bf16[256,2048]{1,0:T(8,128)(2,1)S(1)} %get-tuple-element.4.x_ref, bf16[256,2048]{1,0:T(8,128)(2,1)S(1)} %get-tuple-element.5.input_ref), custom_call_target="tpu_custom_call" | custom-call | tf_op jit(solution)/shard_map/store/pallas_call | solution.py:664

commit v4 on v3

--- a/solution.py
+++ b/solution.py
@@ -10,8 +10,13 @@
 HEAD_DIM = 64
 STATE = 128
 SPAN = 128
-LAG = 5
-WAIT = 6
+FIRST = 8
+SLOT = 2
+HOP = 3
+WAIT = 8
+EDGE_RELAY = 30
+LATER = 6
+INNER_RELAY = 40
 F32 = jnp.float32
 BF16 = jnp.bfloat16
 MESH = pl.DeviceIdType.MESH
@@ -55,9 +60,9 @@
 
 def fused_kernel(
     columns, chips, pieces, whole, lens_ref, x_hbm, dy_hbm, b_hbm, c_hbm, log_hbm, wb_ref, wc_ref, gx_ref, out_ref,
-    x_ref, dy_ref, b_ref, c_ref, log_ref, turned, totals, d_ref, d_prev, d_next, bias, scores, mixed,
+    x_ref, dy_ref, b_ref, c_ref, log_ref, turned, totals, d_ref, d_near, bias, scores, mixed,
     xw_ref, dyw_ref, gx_local, gb_ref, gc_ref, gbc_ref, f0_ref, f_ref, g1_ref, g_ref,
-    c_in, c_out, c_side, b_in, b_out, b_side,
+    chain_in, chain_out, own_out, near_in, mid_out, start_in,
     w_own, w_far, pair_out, pair_in, chip_out, chip_in,
     load_sems, d_sems, send_sems, recv_sems,
     w_sems, pair_send, pair_recv, chip_send, chip_recv,
@@ -93,34 +98,12 @@
     def place(c):
         if not whole:
             return c
-        held = c // 4
-        pair_at = (c - 4 * held) // 2
-        odd = c - 2 * (c // 2)
-        added = (1 - pair_at) * (2 * across + odd) + pair_at * (2 * ((1 - odd) * over_y + odd * over_z) + 1)
-        gathered = (1 - pair_at) * (2 * here + odd) + pair_at * 2 * ((1 - odd) * over_y + odd * over_z)
-        return (1 - held) * added + held * gathered
-
-    barrier = pltpu.get_barrier_semaphore()
-    for offset in (-2, -1, 1, 2):
-        @pl.when(jnp.logical_and(k + offset >= 0, k + offset < devices))
-        def _():
-            pl.semaphore_signal(
-                barrier, inc=1, device_id={"seq": k + offset, "tp": t}, device_id_type=MESH
-            )
-
-    def owner_of(offset, same_core):
-        at = lax.rem(chip + offset, chips)
-        return 2 * at + (core if same_core else 1 - core)
-
-    pl.semaphore_signal(barrier, inc=1, device_id={"seq": k, "tp": mate}, device_id_type=MESH)
-    for offset in range(1, chips):
-        pl.semaphore_signal(
-            barrier, inc=1, device_id={"seq": k, "tp": owner_of(offset, True)}, device_id_type=MESH
-        )
-    if whole:
-        pl.semaphore_signal(
-            barrier, inc=1, device_id={"seq": k, "tp": owner_of(1, False)}, device_id_type=MESH
-        )
+        at = 2 * across
+        for first, value in (
+            (1, 3 - 2 * r), (2, 5), (3, 7), (4, 2 * here), (5, 2 * r + 1), (6, 2 * over_z), (7, 2 * over_y)
+        ):
+            at = jnp.where(c >= first, value, at)
+        return at
 
     quarter = x_ref.shape[1] // 4
     loads = [
@@ -135,6 +118,30 @@
     for load in loads:
         load.start()
 
+    barrier = pltpu.get_barrier_semaphore()
+    pl.semaphore_signal(barrier, inc=1, device_id={"seq": partner, "tp": t}, device_id_type=MESH)
+    for offset in (-2, 2):
+        @pl.when(jnp.logical_and(k + offset >= 0, k + offset < devices))
+        def _():
+            pl.semaphore_signal(
+                barrier, inc=1, device_id={"seq": k + offset, "tp": t}, device_id_type=MESH
+            )
+
+    def owner_of(offset, same_core):
+        at = lax.rem(chip + offset, chips)
+        return 2 * at + (core if same_core else 1 - core)
+
+    pl.semaphore_signal(barrier, inc=1, device_id={"seq": k, "tp": mate}, device_id_type=MESH)
+    for offset in range(1, chips):
+        pl.semaphore_signal(
+            barrier, inc=1, device_id={"seq": k, "tp": owner_of(offset, True)}, device_id_type=MESH
+        )
+    if whole:
+        pl.semaphore_signal(
+            barrier, inc=1, device_id={"seq": k, "tp": owner_of(1, False)}, device_id_type=MESH
+        )
+
+
     def rows_of(offset, same_core, c):
         at = owner_of(offset, same_core) * block + place(c) * piece
         return pl.ds(pl.multiple_of(at, piece), piece)
@@ -162,20 +169,21 @@
             device_id={"seq": k, "tp": mate}, device_id_type=MESH,
         )
 
-    def cross_weights(g, same_core, which):
-        source = 1 if same_core else 0
+    def cross_weights(g, source, which):
+        target = 2 * (1 - chip) + source * core + (1 - source) * (1 - core)
+        at = pl.multiple_of(target * block + place(summed + g) * piece, piece)
         return pltpu.make_async_remote_copy(
-            src_ref=(wb_ref, wc_ref)[which].at[rows_of(1, same_core, summed + g)],
+            src_ref=(wb_ref, wc_ref)[which].at[pl.ds(at, piece)],
             dst_ref=w_cross.at[source, g, :, halves(which)],
             send_sem=cross_sems.at[0], recv_sem=cross_sems.at[1 + g],
-            device_id={"seq": k, "tp": owner_of(1, same_core)}, device_id_type=MESH,
-        )
-
-    def relay_weights(axis, source):
+            device_id={"seq": k, "tp": target}, device_id_type=MESH,
+        )
+
+    def relay_weights(source, g):
         return pltpu.make_async_remote_copy(
-            src_ref=w_cross.at[source, 0], dst_ref=w_cross.at[source, 2 + axis],
-            send_sem=relay_sems.at[0], recv_sem=relay_sems.at[1 + axis],
-            device_id={"seq": z_mate if axis else partner, "tp": t}, device_id_type=MESH,
+            src_ref=w_cross.at[source, 1 if g == 1 else 0], dst_ref=w_cross.at[source, g],
+            send_sem=relay_sems.at[0], recv_sem=relay_sems.at[1 + source if g == 3 else 2 + g],
+            device_id={"seq": partner if g == 3 else z_mate, "tp": t}, device_id_type=MESH,
         )
 
     def group_columns(group, half):
@@ -189,15 +197,6 @@
             send_sem=gbc_sems.at[0], recv_sem=gbc_sems.at[3 + group if kind == 1 else 1 + kind // 2],
             device_id={"seq": k, "tp": owner_of(1, True) if kind == 1 else mate}, device_id_type=MESH,
         )
-
-    for offset in range(chips):
-        for same_core in (False, True):
-            def fetch(c, carry):
-                for which in (0, 1):
-                    w_copy(offset, same_core, c, which).start()
-                return carry
-
-            lax.fori_loop(0, pieces if offset == 0 and same_core else summed, fetch, 0)
 
     loads[0].wait()
     low = lax.broadcasted_iota(jnp.int32, (SPAN, width), 1) < HEAD_DIM
@@ -221,51 +220,48 @@
     for h in range(heads):
         d_ref[h] = both[h : h + 1, :]
 
-    count = jnp.minimum(k, 2) + jnp.minimum(devices - 1 - k, 2) + chips + (1 if whole else 0)
+    count = 1 + jnp.minimum(m, 1) + jnp.minimum(columns - 1 - m, 1) + chips + (1 if whole else 0)
     pl.semaphore_wait(barrier, count)
 
-    def copy(stream, c, source, target, to):
-        rows = pl.ds(pl.multiple_of(c * width, width), width)
+    def copy(kind, way, j, source, target, to):
+        rows = pl.ds(pl.multiple_of(j * width, width), width)
         return pltpu.make_async_remote_copy(
-            src_ref=source.at[rows], dst_ref=target.at[rows],
-            send_sem=send_sems.at[stream], recv_sem=recv_sems.at[stream, c],
+            src_ref=source.at[way, rows], dst_ref=target.at[way, rows],
+            send_sem=send_sems.at[kind, way], recv_sem=recv_sems.at[kind, way, j],
             device_id={"seq": to, "tp": t}, device_id_type=MESH,
         )
 
     def settle(held, sem):
         pltpu.make_async_copy(held, held, sem).wait()
 
-    def decay_copy(stream, target, to):
-        return pltpu.make_async_remote_copy(
-            src_ref=d_ref, dst_ref=target,
-            send_sem=d_sems.at[0, stream], recv_sem=d_sems.at[1, stream],
-            device_id={"seq": to, "tp": t}, device_id_type=MESH,
-        )
-
-    to_next = decay_copy(0, d_prev, k + 1)
-    to_prev = decay_copy(1, d_next, k - 1)
-    sends_next = jnp.logical_and(k + 1 >= 2, k + 1 < devices)
-    sends_prev = jnp.logical_and(k >= 1, k - 1 <= devices - 3)
-
-    @pl.when(sends_next)
-    def _():
-        to_next.start()
-
-    @pl.when(sends_prev)
-    def _():
-        to_prev.start()
+    decays = pltpu.make_async_remote_copy(
+        src_ref=d_ref, dst_ref=d_near, send_sem=d_sems.at[0], recv_sem=d_sems.at[1],
+        device_id={"seq": partner, "tp": t}, device_id_type=MESH,
+    )
+    decays.start()
 
     if whole:
-        for g in range(2):
-            for which in (0, 1):
-                for same_core in (False, True):
-                    cross_weights(g, same_core, which).start()
+        for which in (0, 1):
+            for source in (0, 1):
+                cross_weights(0, source, which).start()
+        for which in (0, 1):
+            cross_weights(1, z_at, which).start()
         for g in range(whole):
             for which in (0, 1):
                 mate_weights(g, which).start()
 
     loads[1].wait()
     loads[2].wait()
+
+    def fetch_weights():
+        for offset in range(chips):
+            for same_core in (False, True):
+                def fetch(c, carry):
+                    for which in (0, 1):
+                        w_copy(offset, same_core, c, which).start()
+                    return carry
+
+                lax.fori_loop(0, pieces if offset == 0 and same_core else summed, fetch, 0)
 
     def spans(number):
         return slice(number * SPAN, (number + 1) * SPAN)
@@ -333,88 +329,116 @@
                 gb_ref[tokens, cols_g] = dot(mixed_low, c_ref[tokens, cols_g], 0, 0)
                 gc_ref[tokens, cols_g] = dot(mixed_low, b_ref[tokens, cols_g], 1, 0)
 
-    def stream(base, has_in, has_next, ahead, source, buf_in, buf_out, buf_side, near, arrival, passes_own):
-        chain = lambda c: copy(base, c, buf_out, buf_in, ahead)
-        side_own = lambda c: copy(base + 1, c, buf_out, buf_side, partner)
-        side_in = lambda c: copy(base + 1, c, buf_in, buf_side, partner)
-        passes_in = jnp.logical_and(jnp.logical_not(passes_own), has_in)
-        side_arrives = jnp.logical_or(jnp.logical_not(passes_own), has_in)
-
-        def step(c):
-            @pl.when(jnp.logical_and(has_in, c == 0))
-            def _():
-                arrival.wait_recv()
-
+    def stream(way, source):
+        first = r == way
+        second = jnp.logical_not(first)
+        has_in = (m < columns - 1) if way else (m > 0)
+        has_next = (m > 0) if way else (m < columns - 1)
+        gives = jnp.logical_or(first, has_next)
+        own = lambda j: copy(0, way, j, own_out, near_in, partner)
+        chain = lambda j: copy(1, way, j, chain_out, chain_in, k - 2 if way else k + 2)
+        middle = lambda j: copy(2, way, j, mid_out, start_in, partner)
+        passed = lambda j: copy(2, way, j, chain_in, start_in, partner)
+
+        @pl.when(jnp.logical_not(has_in))
+        def _():
+            chain_in[way] = jnp.zeros(chain_in.shape[1:], BF16)
+
+        def part(j, e):
+            rows = pl.ds(pl.multiple_of(j * width + e * HEAD_DIM, HEAD_DIM), HEAD_DIM)
+            held = pl.ds(pl.multiple_of((2 * j + r) * width + e * HEAD_DIM, HEAD_DIM), HEAD_DIM)
+            return rows, held, 2 * (2 * j + r) + e
+
+        def give(j):
+            @pl.when(gives)
+            def _():
+                away = pl.ds(pl.multiple_of((2 * j + 1 - r) * width, width), width)
+                own_out[way, j * width : (j + 1) * width] = source[away, :].astype(BF16)
+                own(j).start()
+
+        def step(j):
             @pl.when(has_in)
             def _():
-                chain(c).wait_recv()
-
-                @pl.when(jnp.logical_not(passes_own))
+                chain(j).wait_recv()
+
+            @pl.when(first)
+            def _():
+                for e in range(2):
+                    rows, held, h = part(j, e)
+                    mid_out[way, rows] = (
+                        source[held, :] + d_ref[h] * chain_in[way, rows].astype(F32)
+                    ).astype(BF16)
+                middle(j).start()
+
+                @pl.when(has_next)
                 def _():
-                    side_in(c).start()
+                    own(j).wait_recv()
+                    for e in range(2):
+                        rows, held, h = part(j, e)
+                        mid = source[held, :] + d_ref[h] * chain_in[way, rows].astype(F32)
+                        chain_out[way, rows] = (
+                            near_in[way, rows].astype(F32) + d_near[h] * mid
+                        ).astype(BF16)
+                    chain(j).start()
 
                 for e in range(2):
-                    h = 2 * c + e
-                    rows = pl.ds(pl.multiple_of(h * HEAD_DIM, HEAD_DIM), HEAD_DIM)
-                    product = d_ref[h] * near[h]
-                    buf_out[rows, :] = (source[rows, :] + product * buf_in[rows, :].astype(F32)).astype(BF16)
-
-            @pl.when(jnp.logical_not(has_in))
-            def _():
-                rows = pl.ds(pl.multiple_of(c * width, width), width)
-                buf_out[rows, :] = source[rows, :].astype(BF16)
-
-            @pl.when(passes_own)
-            def _():
-                side_own(c).start()
-
-            @pl.when(has_next)
-            def _():
-                chain(c).start()
-
-        def finish(c):
-            @pl.when(side_arrives)
-            def _():
-                side_own(c).wait_recv()
-
-            for e in range(2):
-                h = 2 * c + e
-                rows = slice(h * HEAD_DIM, (h + 1) * HEAD_DIM)
-
+                    rows, held, h = part(j, e)
+                    source[held, :] = chain_in[way, rows].astype(F32)
+
+            @pl.when(second)
+            def _():
                 @pl.when(has_in)
                 def _():
-                    source[rows, :] = (
-                        buf_side[rows, :].astype(F32) + near[h] * buf_in[rows, :].astype(F32)
+                    passed(j).start()
+
+                own(j).wait_recv()
+
+                @pl.when(has_next)
+                def _():
+                    for e in range(2):
+                        rows, held, h = part(j, e)
+                        mid = near_in[way, rows].astype(F32) + d_near[h] * chain_in[way, rows].astype(F32)
+                        chain_out[way, rows] = (source[held, :] + d_ref[h] * mid).astype(BF16)
+                    chain(j).start()
+
+                for e in range(2):
+                    rows, held, h = part(j, e)
+                    source[held, :] = (
+                        near_in[way, rows].astype(F32) + d_near[h] * chain_in[way, rows].astype(F32)
                     )
 
-                @pl.when(jnp.logical_and(jnp.logical_not(has_in), side_arrives))
-                def _():
-                    source[rows, :] = buf_side[rows, :].astype(F32)
-
-                @pl.when(jnp.logical_not(side_arrives))
-                def _():
-                    source[rows, :] = jnp.zeros((HEAD_DIM, STATE), F32)
+        def finish(c):
+            j = c // 2
+            rows = slice(c * width, (c + 1) * width)
+            away = r == 1 - c % 2
+            arrives = jnp.logical_or(second, has_in)
+
+            @pl.when(jnp.logical_and(away, arrives))
+            def _():
+                middle(j).wait_recv()
+                source[rows, :] = start_in[way, j * width : (j + 1) * width].astype(F32)
+
+            @pl.when(jnp.logical_and(away, jnp.logical_not(arrives)))
+            def _():
+                source[rows, :] = jnp.zeros((width, STATE), F32)
 
         def drain():
+            @pl.when(gives)
+            def _():
+                settle(own_out.at[way], send_sems.at[0, way])
+
             @pl.when(has_next)
             def _():
-                settle(buf_out, send_sems.at[base])
-
-            @pl.when(jnp.logical_or(passes_own, passes_in))
-            def _():
-                settle(buf_out, send_sems.at[base + 1])
-
-        return step, finish, drain
-
-    forward, forward_end, forward_drain = stream(
-        0, m > 0, m < columns - 1, k + 2, f_ref, c_in, c_out, c_side, d_prev, to_next, r == 0
-    )
-    backward, backward_end, backward_drain = stream(
-        2, m < columns - 1, m > 0, k - 2, g_ref, b_in, b_out, b_side, d_next, to_prev, r == 1
-    )
-    lead = LAG * (columns - 1 - 2 * m)
-    forward_at = jnp.maximum(-lead, 0)
-    backward_at = jnp.maximum(lead, 0)
+                settle(chain_out.at[way], send_sems.at[1, way])
+
+            @pl.when(jnp.logical_or(first, has_in))
+            def _():
+                settle(mid_out.at[way], send_sems.at[2, way])
+
+        return give, step, finish, drain
+
+    forward_give, forward, forward_end, forward_drain = stream(0, f_ref)
+    backward_give, backward, backward_end, backward_drain = stream(1, g_ref)
 
     def carried(pair):
         group = pair // pairs
@@ -442,32 +466,74 @@
                     gbc_copy(0, group, half).start()
 
     per_load = max(chunks // 4, 1)
-    span_of_steps = LAG * (columns - 1)
-
-    def exchange(s):
-        f = s - forward_at
-        b = s - backward_at
-
-        @pl.when(jnp.logical_and(f >= 0, f < chunks))
+    rounds = chunks // 2
+    last = HOP * (columns - 1)
+
+    def exchange(e):
+        f = e - HOP * m
+        b = e - HOP * (columns - 1 - m)
+
+        @pl.when(jnp.logical_and(f >= 0, f < rounds))
         def _():
             forward(f)
 
-        @pl.when(jnp.logical_and(b >= 0, b < chunks))
+        @pl.when(jnp.logical_and(b >= 0, b < rounds))
         def _():
             backward(b)
 
-    for s in range(chunks + span_of_steps + WAIT):
+    early = 2 * m < columns
+
+    def give(j, soon):
+        @pl.when(early if soon else jnp.logical_not(early))
+        def _():
+            forward_give(j)
+
+        @pl.when(jnp.logical_not(early) if soon else early)
+        def _():
+            backward_give(j)
+
+    edge = jnp.logical_or(m == 0, m == columns - 1)
+    done = 0
+    for s in range(FIRST + SLOT * (last + rounds) + WAIT):
+        if s == min(3, chunks - 1):
+            fetch_weights()
         if s < chunks:
             if s % per_load == 0:
                 loads[3 + 2 * (s // per_load)].wait()
                 loads[4 + 2 * (s // per_load)].wait()
             summarize(s)
-        if s < chunks + span_of_steps:
-            exchange(s)
-        if s < chunks:
-            local(s)
-        if s >= span_of_steps + WAIT:
-            carried(s - span_of_steps - WAIT)
+            if s % 2:
+                give(s // 2, True)
+        behind = s - LATER
+        if behind >= 0 and behind % 2 == 1 and behind < chunks:
+            give(behind // 2, False)
+        e = (s - FIRST) // SLOT
+        if s >= FIRST and (s - FIRST) % SLOT == 0 and e < last + rounds:
+            if e == 0:
+                decays.wait_recv()
+            exchange(e)
+        if chunks <= s < 2 * chunks:
+            local(s - chunks)
+        if whole and s == EDGE_RELAY:
+            settle(w_cross.at[:, 0], cross_sems.at[1])
+        for at, sends in ((EDGE_RELAY, edge), (INNER_RELAY, jnp.logical_not(edge))):
+            if whole and s == at:
+                @pl.when(sends)
+                def _():
+                    for source in (0, 1):
+                        relay_weights(source, 2).start()
+        if whole and s == INNER_RELAY:
+            settle(w_cross.at[0, 1], cross_sems.at[2])
+            relay_weights(z_at, 1).start()
+        ready = s - FIRST - SLOT * last - WAIT
+        if s >= 2 * chunks - 1 and ready >= 0:
+            while done < chunks and done < 2 * (ready // SLOT + 1):
+                carried(done)
+                done += 1
+    while done < chunks:
+        carried(done)
+        done += 1
+
 
     def relay_group(group):
         settle(gbc_in.at[1, :, pl.ds(0, 2 * STATE)], gbc_sems.at[3 + group])
@@ -478,12 +544,8 @@
     settle(w_far, w_sems.at[1])
 
     if whole:
-        settle(w_cross.at[:, 0], cross_sems.at[1])
         for source in (0, 1):
-            for axis in (0, 1):
-                relay_weights(axis, source).start()
-        for group in range(groups - 1):
-            relay_group(group)
+            relay_weights(source, 3).start()
 
     def pair_copy(offset, c):
         slot = offset * summed + c
@@ -538,18 +600,21 @@
 
     def gather(g, carry):
         total = dot(gbc_ref[...], w_own[summed + g], 1, 1) + dot(gbc_in[0], w_mate[g], 1, 1)
-        total = total + dot(gbc_in[1], w_cross[1, g], 1, 1) + dot(gbc_in[2], w_cross[0, g], 1, 1)
+        for source, held in ((0, gbc_in.at[2]), (1, gbc_in.at[1])):
+            if not isinstance(g, jax.Array) and g == 3:
+                settle(w_cross.at[source, 3], relay_sems.at[1 + source])
+            total = total + dot(held[...], w_cross[source, g], 1, 1)
         cols = pl.ds(pl.multiple_of(place(summed + g) * piece, piece), piece)
         out_ref[:, cols] = total.astype(BF16)
         return carry
 
     if whole:
-        relay_group(groups - 1)
+        for group in range(groups):
+            relay_group(group)
         settle(w_mate, mate_sems.at[1])
-        settle(w_cross.at[:, 1], cross_sems.at[2])
         settle(gbc_in.at[0], gbc_sems.at[1])
         settle(gbc_in.at[2], gbc_sems.at[2])
-        lax.fori_loop(0, 2, gather, 0)
+        gather(0, 0)
 
     def final(c, carry):
         total = partial(0, True, c)
@@ -562,31 +627,27 @@
         out_ref[:, cols] = total.astype(BF16)
         return carry
 
-    early = summed - 1 if whole else summed
-    lax.fori_loop(0, early, final, 0)
+    lax.fori_loop(0, summed - 2 if whole else summed, final, 0)
     if whole:
-        for axis in (0, 1):
-            settle(w_cross.at[:, 2 + axis], relay_sems.at[1 + axis])
-        lax.fori_loop(2, whole, gather, 0)
-        final(early, 0)
+        settle(w_cross.at[:, 2], relay_sems.at[4])
+        gather(2, 0)
+        final(summed - 2, 0)
+        gather(3, 0)
+        settle(w_cross.at[0, 1], relay_sems.at[3])
+        gather(1, 0)
+        final(summed - 1, 0)
 
     settle(pair_out, pair_send.at[0])
     settle(chip_out, chip_send.at[0])
     if whole:
-        settle(w_cross.at[:, pl.ds(0, 2)], cross_sems.at[0])
+        settle(w_cross.at[0, pl.ds(0, 3)], cross_sems.at[0])
         settle(w_mate, mate_sems.at[0])
-        settle(w_cross.at[:, pl.ds(0, 2)], relay_sems.at[0])
+        settle(w_own.at[pl.ds(0, 5)], relay_sems.at[0])
         settle(gbc_in, gbc_sems.at[0])
     forward_drain()
     backward_drain()
 
-    @pl.when(sends_next)
-    def _():
-        to_next.wait_send()
-
-    @pl.when(sends_prev)
-    def _():
-        to_prev.wait_send()
+    decays.wait_send()
 
 
 def store_kernel(x_ref, input_ref, x_hbm, input_hbm, sems):
@@ -632,14 +693,14 @@
             vmem((tokens, wide), BF16), vmem((tokens, wide), BF16),
             vmem((heads, tokens), F32),
             vmem((6, SPAN, heads), F32), vmem((2, heads, SPAN), F32),
-            row, row, row,
+            row, row,
             square(2), square(2 * groups), square(2 * groups),
             vmem((tokens, inner), BF16), vmem((tokens, inner), BF16),
             vmem((tokens, inner), F32),
             vmem((tokens, wide), F32), vmem((tokens, wide), F32), vmem((tokens, 2 * wide), BF16),
         ]
         + [vmem((inner, STATE), F32)] * 4
-        + [vmem((inner, STATE), BF16)] * 6
+        + [vmem((2, inner // 2, STATE), BF16)] * 6
         + [
             vmem((pieces, piece, 2 * wide), BF16),
             vmem(((2 * chips - 1) * summed, piece, 2 * wide), BF16),
@@ -647,14 +708,14 @@
             vmem((chips * summed, tokens, piece), BF16),
             vmem(((chips - 1) * summed, tokens, piece), BF16),
             vmem(((chips - 1) * summed, tokens, piece), BF16),
-            dma((11,)), dma((2, 2)), dma((4,)), dma((4, chunks)),
+            dma((11,)), dma((2,)), dma((3, 2)), dma((3, 2, chunks // 2)),
             dma((2,)), dma((1,)), dma((chips * summed,)), dma((1,)), dma(((chips - 1) * summed,)),
         ]
         + ([
             vmem((whole, piece, 2 * wide), BF16),
             vmem((2, whole, piece, 2 * wide), BF16),
             vmem((3, tokens, 2 * wide), BF16),
-            dma((2,)), dma((3,)), dma((3,)), dma((3 + groups,)),
+            dma((2,)), dma((3,)), dma((5,)), dma((3 + groups,)),
         ] if whole else []),
         compiler_params=pltpu.CompilerParams(
             collective_id=0, has_side_effects=True, vmem_limit_bytes=56 * 1024 * 1024

time: 50.7 us -> 48.7 us (0.961); the launches traced: 49.8 us -> 48.6 us
  Pallas kernels: 49 us -> 47.8 us
    pallas_call x1, Pallas kernels: 47.6 us -> 46.4 us  [per_device(): pl.pallas_call(functools.partial(fused_kernel, seq_count // 2, chips, pie...]
where the time goes in v4:
time: 48.7 us; the launch traced here: 48.6 us
  Pallas kernels  47.8 us (98%)
  between operations  0.8 us (2%)
    pallas_call x1, Pallas kernels, per_device(): pl.pallas_call(functools.partial(fused_kernel, seq_count // 2, chips, pie...  46.4 us
    pallas_call x1, Pallas kernels, per_device(): pl.pallas_call(store_kernel, out_shape=[jax.ShapeDtypeStruct((tokens, inn...  1.38 us

profile of v4, /device:TPU:0, one launch (start us, length us, event | category | flops | bytes accessed | tf_op | source)
XLA Modules:
  0.0 48.6 jit_solution(17008048237949206375)
XLA Ops:
  0.6 46.4 %fused.1 = (bf16[256,2048]{1,0:T(8,128)(2,1)S(1)}, bf16[256,2048]{1,0:T(8,128)(2,1)S(1)}) custom-call(s32[4]{0:T(128)} %lens_ref.1, bf16[256,2048]{1,0:T(8,128)(2,1)} %x_hbm.1, bf16[256,2048]{1,0:T(8,128)(2,1)} %dy_hbm.1, bf16[256,256]{1,0:T(8,128)(2,1)} %b_hbm.1, bf16[256,256]{1,0:T(8,128)(2,1)} %c_hbm.1, f32[32,256]{1,0:T(8,128)} %log_hbm.1, ...), custom_call_target="tpu_custom_call" | custom-call | tf_op jit(solution)/shard_map/fused/pallas_call | solution.py:683
  47.0 1.4 %store.1 = (bf16[256,2048]{1,0:T(8,128)(2,1)}, bf16[256,2048]{1,0:T(8,128)(2,1)}) custom-call(bf16[256,2048]{1,0:T(8,128)(2,1)S(1)} %get-tuple-element.4.x_ref, bf16[256,2048]{1,0:T(8,128)(2,1)S(1)} %get-tuple-element.5.input_ref), custom_call_target="tpu_custom_call" | custom-call | tf_op jit(solution)/shard_map/store/pallas_call | solution.py:725

commit v5 on v4

--- a/solution.py
+++ b/solution.py
@@ -16,7 +16,7 @@
 WAIT = 8
 EDGE_RELAY = 30
 LATER = 6
-INNER_RELAY = 40
+INNER_RELAY = 36
 F32 = jnp.float32
 BF16 = jnp.bfloat16
 MESH = pl.DeviceIdType.MESH
@@ -70,7 +70,9 @@
 ):
     summed = pieces - whole
     if whole:
-        w_mate, w_cross, gbc_in, mate_sems, cross_sems, relay_sems, gbc_sems = shared
+        w_mate, w_cross, gbc_in, mate_sems, cross_sems, relay_sems, gbc_sems = shared[:7]
+        mate_part, cross_part, pair_part_out, pair_part_in, chip_part_out, chip_part_in, part_sems = shared[7:]
+    lead = summed - 1 if whole else summed
     heads = log_ref.shape[0]
     groups = b_ref.shape[1] // STATE
     chunks = heads // 2
@@ -179,6 +181,17 @@
             device_id={"seq": k, "tp": target}, device_id_type=MESH,
         )
 
+    def part_weights(source, which):
+        target = mate if source is None else 2 * (1 - chip) + source * core + (1 - source) * (1 - core)
+        at = pl.multiple_of(target * block + place(lead) * piece + piece // 2, piece // 2)
+        to = mate_part if source is None else cross_part.at[source]
+        first = 2 if source is None else 0
+        return pltpu.make_async_remote_copy(
+            src_ref=(wb_ref, wc_ref)[which].at[pl.ds(at, piece // 2)], dst_ref=to.at[:, halves(which)],
+            send_sem=part_sems.at[first], recv_sem=part_sems.at[first + 1],
+            device_id={"seq": k, "tp": target}, device_id_type=MESH,
+        )
+
     def relay_weights(source, g):
         return pltpu.make_async_remote_copy(
             src_ref=w_cross.at[source, 1 if g == 1 else 0], dst_ref=w_cross.at[source, g],
@@ -246,6 +259,9 @@
                 cross_weights(0, source, which).start()
         for which in (0, 1):
             cross_weights(1, z_at, which).start()
+        for which in (0, 1):
+            for source in (0, 1, None):
+                part_weights(source, which).start()
         for g in range(whole):
             for which in (0, 1):
                 mate_weights(g, which).start()
@@ -548,7 +564,7 @@
             relay_weights(source, 3).start()
 
     def pair_copy(offset, c):
-        slot = offset * summed + c
+        slot = offset * lead + c
         return pltpu.make_async_remote_copy(
             src_ref=pair_out.at[slot], dst_ref=pair_in.at[slot],
             send_sem=pair_send.at[0], recv_sem=pair_recv.at[slot],
@@ -556,7 +572,7 @@
         )
 
     def chip_copy(offset, c):
-        slot = (offset - 1) * summed + c
+        slot = (offset - 1) * lead + c
         return pltpu.make_async_remote_copy(
             src_ref=chip_out.at[slot], dst_ref=chip_in.at[slot],
             send_sem=chip_send.at[0], recv_sem=chip_recv.at[slot],
@@ -568,19 +584,43 @@
         return dot(gbc_ref[...], weights, 1, 1)
 
     def give(offset, c):
-        pair_out[offset * summed + c] = partial(offset, False, c).astype(BF16)
+        pair_out[offset * lead + c] = partial(offset, False, c).astype(BF16)
         pair_copy(offset, c).start()
 
     def send_on(offset, c):
         own = partial(offset, True, c)
         pair_copy(offset, c).wait_recv()
-        slot = offset * summed + c
-        chip_out[(offset - 1) * summed + c] = (own + pair_in[slot].astype(F32)).astype(BF16)
+        slot = offset * lead + c
+        chip_out[(offset - 1) * lead + c] = (own + pair_in[slot].astype(F32)).astype(BF16)
         chip_copy(offset, c).start()
+
+    def pair_part(offset):
+        return pltpu.make_async_remote_copy(
+            src_ref=pair_part_out.at[offset], dst_ref=pair_part_in.at[offset],
+            send_sem=part_sems.at[4], recv_sem=part_sems.at[5 + offset],
+            device_id={"seq": k, "tp": mate}, device_id_type=MESH,
+        )
+
+    def chip_part():
+        return pltpu.make_async_remote_copy(
+            src_ref=chip_part_out, dst_ref=chip_part_in,
+            send_sem=part_sems.at[7], recv_sem=part_sems.at[8],
+            device_id={"seq": k, "tp": owner_of(1, True)}, device_id_type=MESH,
+        )
+
+    low_rows, high_rows = pl.ds(0, piece // 2), pl.ds(piece // 2, piece // 2)
+
+    def give_part(offset):
+        weights = w_far[far_slot(offset, False, lead), low_rows]
+        pair_part_out[offset] = dot(gbc_ref[...], weights, 1, 1).astype(BF16)
+        pair_part(offset).start()
+
+    if whole:
+        give_part(1)
 
     for offset in range(1, chips):
         def body(s, carry):
-            @pl.when(s < summed)
+            @pl.when(s < lead)
             def _():
                 give(offset, s)
 
@@ -590,13 +630,21 @@
 
             return carry
 
-        lax.fori_loop(0, summed + 2, body, 0)
+        lax.fori_loop(0, lead + 2, body, 0)
+
+    if whole:
+        own = dot(gbc_ref[...], w_far[far_slot(1, True, lead), low_rows], 1, 1)
+        pair_part(1).wait_recv()
+        chip_part_out[...] = (own + pair_part_in[1].astype(F32)).astype(BF16)
+        chip_part().start()
 
     def near_give(c, carry):
         give(0, c)
         return carry
 
-    lax.fori_loop(0, summed, near_give, 0)
+    lax.fori_loop(0, lead, near_give, 0)
+    if whole:
+        give_part(0)
 
     def gather(g, carry):
         total = dot(gbc_ref[...], w_own[summed + g], 1, 1) + dot(gbc_in[0], w_mate[g], 1, 1)
@@ -615,6 +663,12 @@
         settle(gbc_in.at[0], gbc_sems.at[1])
         settle(gbc_in.at[2], gbc_sems.at[2])
         gather(0, 0)
+        settle(mate_part, part_sems.at[3])
+        settle(cross_part, part_sems.at[1])
+        total = dot(gbc_ref[...], w_own[lead, high_rows], 1, 1) + dot(gbc_in[0], mate_part[...], 1, 1)
+        total = total + dot(gbc_in[2], cross_part[0], 1, 1) + dot(gbc_in[1], cross_part[1], 1, 1)
+        split = place(lead) * piece
+        out_ref[:, pl.ds(pl.multiple_of(split + piece // 2, piece // 2), piece // 2)] = total.astype(BF16)
 
     def final(c, carry):
         total = partial(0, True, c)
@@ -622,26 +676,35 @@
         total = total + pair_in[c].astype(F32)
         for offset in range(1, chips):
             chip_copy(offset, c).wait_recv()
-            total = total + chip_in[(offset - 1) * summed + c].astype(F32)
+            total = total + chip_in[(offset - 1) * lead + c].astype(F32)
         cols = pl.ds(pl.multiple_of(place(c) * piece, piece), piece)
         out_ref[:, cols] = total.astype(BF16)
         return carry
 
-    lax.fori_loop(0, summed - 2 if whole else summed, final, 0)
+    lax.fori_loop(0, lead - 1 if whole else lead, final, 0)
     if whole:
         settle(w_cross.at[:, 2], relay_sems.at[4])
         gather(2, 0)
-        final(summed - 2, 0)
-        gather(3, 0)
         settle(w_cross.at[0, 1], relay_sems.at[3])
         gather(1, 0)
-        final(summed - 1, 0)
+        final(lead - 1, 0)
+        gather(3, 0)
+        total = dot(gbc_ref[...], w_own[lead, low_rows], 1, 1)
+        pair_part(0).wait_recv()
+        total = total + pair_part_in[0].astype(F32)
+        chip_part().wait_recv()
+        total = total + chip_part_in[...].astype(F32)
+        out_ref[:, pl.ds(pl.multiple_of(split, piece // 2), piece // 2)] = total.astype(BF16)
 
     settle(pair_out, pair_send.at[0])
     settle(chip_out, chip_send.at[0])
     if whole:
         settle(w_cross.at[0, pl.ds(0, 3)], cross_sems.at[0])
         settle(w_mate, mate_sems.at[0])
+        settle(cross_part, part_sems.at[0])
+        settle(mate_part, part_sems.at[2])
+        settle(pair_part_out, part_sems.at[4])
+        settle(chip_part_out, part_sems.at[7])
         settle(w_own.at[pl.ds(0, 5)], relay_sems.at[0])
         settle(gbc_in, gbc_sems.at[0])
     forward_drain()
@@ -653,8 +716,8 @@
 def store_kernel(x_ref, input_ref, x_hbm, input_hbm, sems):
     copies = []
     for i, (held, target) in enumerate(((x_ref, x_hbm), (input_ref, input_hbm))):
-        part = held.shape[0] // 4
-        for n in range(4):
+        part = held.shape[0]
+        for n in range(1):
             rows = pl.ds(n * part, part)
             copies.append(pltpu.make_async_copy(held.at[rows], target.at[rows], sems.at[i, n]))
     for copy in copies:
@@ -675,6 +738,7 @@
     wide = in_b.shape[1]
     whole = 4 if chips == 2 and pieces == 8 and seq_count % 4 == 0 else 0
     summed = pieces - whole
+    lead = summed - 1 if whole else summed
     groups = wide // STATE
     vmem = pltpu.VMEM
     dma = pltpu.SemaphoreType.DMA
@@ -704,18 +768,21 @@
         + [
             vmem((pieces, piece, 2 * wide), BF16),
             vmem(((2 * chips - 1) * summed, piece, 2 * wide), BF16),
-            vmem((chips * summed, tokens, piece), BF16),
-            vmem((chips * summed, tokens, piece), BF16),
-            vmem(((chips - 1) * summed, tokens, piece), BF16),
-            vmem(((chips - 1) * summed, tokens, piece), BF16),
+            vmem((chips * lead, tokens, piece), BF16),
+            vmem((chips * lead, tokens, piece), BF16),
+            vmem(((chips - 1) * lead, tokens, piece), BF16),
+            vmem(((chips - 1) * lead, tokens, piece), BF16),
             dma((11,)), dma((2,)), dma((3, 2)), dma((3, 2, chunks // 2)),
-            dma((2,)), dma((1,)), dma((chips * summed,)), dma((1,)), dma(((chips - 1) * summed,)),
+            dma((2,)), dma((1,)), dma((chips * lead,)), dma((1,)), dma(((chips - 1) * lead,)),
         ]
         + ([
             vmem((whole, piece, 2 * wide), BF16),
             vmem((2, whole, piece, 2 * wide), BF16),
             vmem((3, tokens, 2 * wide), BF16),
             dma((2,)), dma((3,)), dma((5,)), dma((3 + groups,)),
+            vmem((piece // 2, 2 * wide), BF16), vmem((2, piece // 2, 2 * wide), BF16),
+            vmem((chips, tokens, piece // 2), BF16), vmem((chips, tokens, piece // 2), BF16),
+            vmem((tokens, piece // 2), BF16), vmem((tokens, piece // 2), BF16), dma((9,)),
         ] if whole else []),
         compiler_params=pltpu.CompilerParams(
             collective_id=0, has_side_effects=True, vmem_limit_bytes=56 * 1024 * 1024
@@ -730,7 +797,7 @@
         ],
         in_specs=[pl.BlockSpec(memory_space=vmem)] * 2,
         out_specs=[ANY] * 2,
-        scratch_shapes=[dma((2, 4))],
+        scratch_shapes=[dma((2, 1))],
         name="store",
     )(pltpu.with_memory_space_constraint(held_x, pltpu.VMEM), pltpu.with_memory_space_constraint(held_input, pltpu.VMEM)))
 

time: 48.7 us -> 48 us (0.986)
  Pallas kernels: 47.8 us -> 47 us
    pallas_call x1, Pallas kernels: 46.4 us -> 45.7 us  [per_device(): pl.pallas_call(functools.partial(fused_kernel, seq_count // 2, chips, pie...]
where the time goes in v5:
time: 48 us; the launch traced here: 47.8 us
  Pallas kernels  47 us (98%)
  between operations  0.8 us (2%)
    pallas_call x1, Pallas kernels, per_device(): pl.pallas_call(functools.partial(fused_kernel, seq_count // 2, chips, pie...  45.7 us
    pallas_call x1, Pallas kernels, per_device(): pl.pallas_call(store_kernel, out_shape=[jax.ShapeDtypeStruct((tokens, inn...  1.33 us

profile of v5, /device:TPU:0, one launch (start us, length us, event | category | flops | bytes accessed | tf_op | source)
XLA Modules:
  0.0 47.8 jit_solution(8888323765156740510)
XLA Ops:
  0.6 45.7 %fused.1 = (bf16[256,2048]{1,0:T(8,128)(2,1)S(1)}, bf16[256,2048]{1,0:T(8,128)(2,1)S(1)}) custom-call(s32[4]{0:T(128)} %lens_ref.1, bf16[256,2048]{1,0:T(8,128)(2,1)} %x_hbm.1, bf16[256,2048]{1,0:T(8,128)(2,1)} %dy_hbm.1, bf16[256,256]{1,0:T(8,128)(2,1)} %b_hbm.1, bf16[256,256]{1,0:T(8,128)(2,1)} %c_hbm.1, f32[32,256]{1,0:T(8,128)} %log_hbm.1, ...), custom_call_target="tpu_custom_call" | custom-call | tf_op jit(solution)/shard_map/fused/pallas_call | solution.py:747
  46.3 1.3 %store.1 = (bf16[256,2048]{1,0:T(8,128)(2,1)}, bf16[256,2048]{1,0:T(8,128)(2,1)}) custom-call(bf16[256,2048]{1,0:T(8,128)(2,1)S(1)} %get-tuple-element.4.x_ref, bf16[256,2048]{1,0:T(8,128)(2,1)S(1)} %get-tuple-element.5.input_ref), custom_call_target="tpu_custom_call" | custom-call | tf_op jit(solution)/shard_map/store/pallas_call | solution.py:792

commit v6 on v5

--- a/solution.py
+++ b/solution.py
@@ -10,7 +10,7 @@
 HEAD_DIM = 64
 STATE = 128
 SPAN = 128
-FIRST = 8
+FIRST = 9
 SLOT = 2
 HOP = 3
 WAIT = 8
@@ -259,12 +259,6 @@
                 cross_weights(0, source, which).start()
         for which in (0, 1):
             cross_weights(1, z_at, which).start()
-        for which in (0, 1):
-            for source in (0, 1, None):
-                part_weights(source, which).start()
-        for g in range(whole):
-            for which in (0, 1):
-                mate_weights(g, which).start()
 
     loads[1].wait()
     loads[2].wait()
@@ -513,6 +507,13 @@
     for s in range(FIRST + SLOT * (last + rounds) + WAIT):
         if s == min(3, chunks - 1):
             fetch_weights()
+            if whole:
+                for which in (0, 1):
+                    for source in (0, 1, None):
+                        part_weights(source, which).start()
+                for g in range(whole):
+                    for which in (0, 1):
+                        mate_weights(g, which).start()
         if s < chunks:
             if s % per_load == 0:
                 loads[3 + 2 * (s // per_load)].wait()

time: 48 us -> 47.7 us (level)
  no operation moved by 1% of the time
where the time goes in v6:
time: 47.7 us; the launch traced here: 47.6 us
  Pallas kernels  46.8 us (98%)
  between operations  0.8 us (2%)
    pallas_call x1, Pallas kernels, per_device(): pl.pallas_call(functools.partial(fused_kernel, seq_count // 2, chips, pie...  45.4 us
    pallas_call x1, Pallas kernels, per_device(): pl.pallas_call(store_kernel, out_shape=[jax.ShapeDtypeStruct((tokens, inn...  1.33 us

profile of v6, /device:TPU:0, one launch (start us, length us, event | category | flops | bytes accessed | tf_op | source)
XLA Modules:
  0.0 47.6 jit_solution(4116219131939967211)
XLA Ops:
  0.6 45.4 %fused.1 = (bf16[256,2048]{1,0:T(8,128)(2,1)S(1)}, bf16[256,2048]{1,0:T(8,128)(2,1)S(1)}) custom-call(s32[4]{0:T(128)} %lens_ref.1, bf16[256,2048]{1,0:T(8,128)(2,1)} %x_hbm.1, bf16[256,2048]{1,0:T(8,128)(2,1)} %dy_hbm.1, bf16[256,256]{1,0:T(8,128)(2,1)} %b_hbm.1, bf16[256,256]{1,0:T(8,128)(2,1)} %c_hbm.1, f32[32,256]{1,0:T(8,128)} %log_hbm.1, ...), custom_call_target="tpu_custom_call" | custom-call | tf_op jit(solution)/shard_map/fused/pallas_call | solution.py:748
  46.1 1.3 %store.1 = (bf16[256,2048]{1,0:T(8,128)(2,1)}, bf16[256,2048]{1,0:T(8,128)(2,1)}) custom-call(bf16[256,2048]{1,0:T(8,128)(2,1)S(1)} %get-tuple-element.4.x_ref, bf16[256,2048]{1,0:T(8,128)(2,1)S(1)} %get-tuple-element.5.input_ref), custom_call_target="tpu_custom_call" | custom-call | tf_op jit(solution)/shard_map/store/pallas_call | solution.py:793
